TPU v7x, 128 devices: a whole 4x4x4 slice. The times are simulated.
128 devices in a mesh: rows: 4 (over z), vocab: 32 (over x, y, core).
Axes of the slice: x: 4, y: 4, z: 4, core: 2. Of those that a mesh axis runs over, the one named last changes fastest.
Arguments:
- expert_delta: bfloat16 [512, 32000], P(None, ('rows', 'vocab')), may hold values from -24 to 24
- small_anchors: bfloat16 [32000, 2048], P(('rows', 'vocab')), may hold values from -0.18 to 0.18
- small_tokens: int32 [2048], replicated, may hold values from 0 to 31999, as said below
- base_logits: float32 [512, 128256], P('rows', 'vocab'), may hold values from -2 to 300
- base_anchors: bfloat16 [128256, 2048], P('vocab'), may hold values from -0.18 to 0.18
- base_tokens: int32 [2048], replicated, may hold values from 0 to 128255, as said below
- active_rows: int32 [512], P('rows'), may hold values 0 or 1
Outputs:
- logit_update: float32 [512, 128256], P('rows', 'vocab')
Inputs may be any that keep to these rules, and one draw needn't show every extreme that they name: `small_tokens`: 2048 distinct token ids, the first and last ids of the small vocabulary among them. `base_tokens`: 2048 distinct token ids, the first and last ids of the base vocabulary among them.
All inputs are finite; a program needn't handle non-finite values. No bound on the sum of `active_rows` on one device may be relied on, other than what follows from the above.
Results may differ from a plain program's by a relative error of at most 0.03.
Values may be sent and summed in bfloat16 or wider, within the bound.
No kernel may reach another device: no remote copies, remote signals or barrier semaphores. Data moves between devices by JAX's collectives and lax.ppermute only.
A program may use at most 128 MiB of HBM per device.

v0:
```python
import functools
import jax
import jax.numpy as jnp
from jax import lax
from jax.experimental import pallas as pl
from jax.experimental.pallas import tpu as pltpu
from jax.sharding import Mesh
from jax.sharding import PartitionSpec as P

ITERATIONS = 3
VOCAB = ("x", "y", "core")
CHIPS = ("rows", "x", "y")
LANES = 128
CHUNK = 512
epsilon = 1e-06
step_size = 2.0

HBM = pl.BlockSpec(memory_space=pl.ANY)
VMEM = pl.BlockSpec(memory_space=pltpu.VMEM)
SMEM = pl.BlockSpec(memory_space=pltpu.SMEM)


def chunks_of(extent):
    starts = list(range(0, extent, CHUNK))
    return [(start, min(CHUNK, extent - start)) for start in starts]


def three_parts(value):
    high = value.astype(jnp.bfloat16).astype(jnp.float32)
    rest = value - high
    middle = rest.astype(jnp.bfloat16).astype(jnp.float32)
    return high, middle, rest - middle


def matmul_nt(left, right):
    return lax.dot_general(left, right, (((1,), (1,)), ((), ())), preferred_element_type=jnp.float32)


def with_self(block, tokens, start):
    rows, columns = block.shape
    if rows % 16 == 0:
        place = lax.broadcasted_iota(jnp.int16, (rows, columns), 0) + jnp.int16(start)
        wanted = jnp.broadcast_to(tokens[None], (rows // 16, 16, columns)).reshape(rows, columns)
    else:
        place = lax.broadcasted_iota(jnp.int16, (rows, columns), 0) + jnp.int16(start)
        whole = -(-rows // 16)
        wanted = jnp.broadcast_to(tokens[None], (whole, 16, columns)).reshape(whole * 16, columns)[:rows]
    return jnp.where(place == wanted, block + jnp.bfloat16(1), block)


def put_masses(logits_ref, anchors_of, out_ref, mass_ref):
    extent, rows = logits_ref.shape
    top = jnp.max(logits_ref[...], axis=0, keepdims=True)
    total = jnp.zeros((1, rows), jnp.float32)
    for start, size in chunks_of(extent):
        weights = jnp.exp(logits_ref[pl.ds(start, size), :] - top)
        total = total + jnp.sum(weights, axis=0, keepdims=True)
        turned = weights.T.astype(jnp.bfloat16)
        part = jnp.dot(turned, anchors_of(start, size), preferred_element_type=jnp.float32)
        if start == 0:
            mass_ref[...] = part
        else:
            mass_ref[...] += part
    groups, halves, eight, width = out_ref.shape
    half = width - LANES
    for h in range(halves):
        piece = mass_ref[:, h * half : (h + 1) * half].reshape(groups, eight, half)
        out_ref[:, h, :, :half] = piece.astype(jnp.bfloat16)
    parts = three_parts(top) + three_parts(total)
    stats = jnp.concatenate(list(parts) + [jnp.zeros((LANES - len(parts), rows), jnp.float32)], axis=0)
    stats = stats.T.reshape(groups, eight, LANES).astype(jnp.bfloat16)
    for h in range(halves):
        out_ref[:, h, :, half:] = stats


def first_kernel(tokens_ref, anchors_ref, logits_ref, held_ref, out_ref, buffer, mass_ref, sem_in, sem_out):
    extent = logits_ref.shape[0]
    pieces = chunks_of(extent)
    loads = []
    for i, (start, size) in enumerate(pieces):
        where = pl.ds(start, size)
        load = pltpu.make_async_copy(anchors_ref.at[where], buffer.at[where], sem_in.at[i])
        load.start()
        loads.append(load)
    stores = []

    def anchors_of(start, size):
        i = start // CHUNK
        where = pl.ds(start, size)
        loads[i].wait()
        block = with_self(buffer[where, :], tokens_ref[...], start)
        buffer[where, :] = block
        store = pltpu.make_async_copy(buffer.at[where], held_ref.at[where], sem_out.at[i])
        store.start()
        stores.append(store)
        return buffer[where, :]

    put_masses(logits_ref, anchors_of, out_ref, mass_ref)
    for store in stores:
        store.wait()


def owner_kernel(full_vocab, target_pieces, in_ref, target_ref, out_ref, sum_ref=None):
    half = in_ref.shape[2] - LANES
    if target_pieces:
        target = jnp.sum(target_ref[...].astype(jnp.float32), axis=0)
        sum_ref[...] = target
    else:
        target = target_ref[...]
    stats = in_ref[:, :, half:].astype(jnp.float32)
    lane = lax.broadcasted_iota(jnp.int32, stats.shape, 2)
    top = jnp.sum(jnp.where(lane < 3, stats, 0.0), axis=2, keepdims=True)
    part = jnp.sum(jnp.where((lane >= 3) & (lane < 6), stats, 0.0), axis=2, keepdims=True)
    row_max = jnp.max(top, axis=0, keepdims=True)
    factor = jnp.exp(top - row_max)
    total = jnp.sum(part * factor, axis=0)
    mass = jnp.sum(in_ref[:, :, :half].astype(jnp.float32) * factor, axis=0)
    gap = full_vocab * mass / total - target
    sent = gap.astype(jnp.bfloat16)
    squares = jnp.sum(gap * gap, axis=1, keepdims=True)
    inner = jnp.sum(sent.astype(jnp.float32) * mass, axis=1, keepdims=True)
    lane = lax.broadcasted_iota(jnp.int32, (in_ref.shape[1], LANES), 1)
    tile = jnp.zeros((in_ref.shape[1], LANES), jnp.float32)
    parts = three_parts(row_max[0]) + three_parts(total) + three_parts(squares) + three_parts(inner)
    for i, value in enumerate(parts):
        tile = jnp.where(lane == i, value, tile)
    out_ref[:, :, :half] = jnp.broadcast_to(sent[None], (in_ref.shape[0],) + sent.shape)
    out_ref[:, :, half:] = jnp.broadcast_to(tile.astype(jnp.bfloat16)[None], (in_ref.shape[0],) + tile.shape)


def step_kernel(last, gap_ref, active_ref, base_ref, update_ref, held_ref, *rest):
    if last:
        new_ref, buffer, gap_all, sem_in = rest
    else:
        new_ref, out_ref, buffer, gap_all, logits_ref, mass_ref, sem_in = rest
    extent, rows = base_ref.shape
    loads = []
    for i, (start, size) in enumerate(chunks_of(extent)):
        where = pl.ds(start, size)
        load = pltpu.make_async_copy(held_ref.at[where], buffer.at[where], sem_in.at[i])
        load.start()
        loads.append(load)
    groups, halves, eight, width = gap_ref.shape
    half = width - LANES
    for h in range(halves):
        piece = gap_ref[:, h, :, :half].astype(jnp.float32).reshape(rows, half)
        gap_all[:, h * half : (h + 1) * half] = piece.astype(jnp.bfloat16)
    stats = [gap_ref[:, h, :, half:].astype(jnp.float32).reshape(rows, LANES).T for h in range(halves)]

    def joined(which, h):
        return jnp.sum(stats[h][3 * which : 3 * which + 3], axis=0, keepdims=True)

    row_max, total = joined(0, 0), joined(1, 0)
    squares = joined(2, 0) + joined(2, 1)
    inner = joined(3, 0) + joined(3, 1)
    scale = lax.rsqrt(squares / (halves * half) + epsilon)
    slope = scale * inner / total
    active = active_ref[...]
    for i, (start, size) in enumerate(chunks_of(extent)):
        where = pl.ds(start, size)
        loads[i].wait()
        back = matmul_nt(buffer[where, :], gap_all[...]) * scale
        logits = base_ref[where, :]
        if update_ref is not None:
            logits = logits + update_ref[where, :]
        weights = jnp.exp(logits - row_max)
        change = -step_size * active * weights * (back - slope)
        new_ref[where, :] = change if update_ref is None else update_ref[where, :] + change
        if not last:
            logits_ref[where, :] = logits + change
    if not last:
        put_masses(logits_ref, lambda start, size: buffer[pl.ds(start, size), :], out_ref, mass_ref)


def no_update(kernel):
    def run(gap_ref, active_ref, base_ref, held_ref, *rest):
        kernel(gap_ref, active_ref, base_ref, None, held_ref, *rest)

    return run


def target_kernel(core_ref, tokens_ref, delta_ref, anchors_ref, mine_ref, other_ref):
    extent, columns = anchors_ref.shape
    half = columns // 2
    delta = delta_ref[...]

    def product(which):
        where = pl.ds(pl.multiple_of(which * half, half), half)
        block = anchors_ref[:, where].astype(jnp.float32)
        place = lax.broadcasted_iota(jnp.int32, (extent, half), 0)
        block = jnp.where(place == tokens_ref[:, where], block + 1.0, block).astype(jnp.bfloat16)
        return jnp.dot(delta, block, preferred_element_type=jnp.float32)

    core = core_ref[0]
    other_ref[...] = product(1 - core).astype(jnp.bfloat16)
    mine_ref[...] = product(core)


def shards(expert_delta, small_anchors, small_tokens, base_logits, base_anchors, base_tokens, active_rows):
    f32, bf16 = jnp.float32, jnp.bfloat16
    vocab_count = lax.axis_size(VOCAB)
    vocab_place = lax.axis_index(VOCAB)
    place = lax.axis_index("rows") * vocab_count + vocab_place
    all_rows, small_width = expert_delta.shape
    base_width, anchors = base_anchors.shape
    rows = base_logits.shape[0]
    half = anchors // 2
    width = half + LANES
    eight = 2 * rows // vocab_count
    groups = vocab_count // 2
    pieces = len(chunks_of(base_width))
    params = pltpu.CompilerParams(vmem_limit_bytes=50 * 1024 * 1024)

    core = lax.axis_index("core").reshape(1)
    small_ids = (small_tokens - place * small_width)[None, :]
    shifted = base_tokens - vocab_place * base_width
    shifted = jnp.where((shifted >= 0) & (shifted < base_width), shifted, -1).astype(jnp.int16)
    base_ids = jnp.broadcast_to(shifted[None, :], (16, anchors))
    active = active_rows.astype(f32)[None, :]
    base = base_logits.T

    mine, other = pl.pallas_call(
        target_kernel,
        out_shape=(jax.ShapeDtypeStruct((all_rows, half), f32), jax.ShapeDtypeStruct((all_rows, half), bf16)),
        in_specs=[SMEM, VMEM, VMEM, VMEM],
        out_specs=(VMEM, VMEM),
        compiler_params=params,
        name="target_parts",
    )(core, small_ids, expert_delta, small_anchors)
    other = lax.ppermute(other, "core", [(0, 1), (1, 0)])
    target = (mine + other.astype(f32)).astype(bf16)
    target = target.reshape(-1, eight, half)
    target = lax.all_to_all(target, CHIPS, 0, 0, tiled=True)

    sent_shape = jax.ShapeDtypeStruct((groups, 2, eight, width), bf16)
    held_shape = jax.ShapeDtypeStruct((base_width, anchors), bf16)
    update_shape = jax.ShapeDtypeStruct((base_width, rows), f32)
    held, sent = pl.pallas_call(
        first_kernel,
        out_shape=(held_shape, sent_shape),
        in_specs=[VMEM, HBM, VMEM],
        out_specs=(HBM, VMEM),
        scratch_shapes=[
            pltpu.VMEM((base_width, anchors), bf16),
            pltpu.VMEM((rows, anchors), f32),
            pltpu.SemaphoreType.DMA((pieces,)),
            pltpu.SemaphoreType.DMA((pieces,)),
        ],
        compiler_params=params,
        name="first_masses",
    )(base_ids, base_anchors, base)

    update = None
    for turn in range(ITERATIONS):
        last = turn == ITERATIONS - 1
        got = lax.all_to_all(sent.reshape(vocab_count, eight, width), VOCAB, 0, 0, tiled=True)
        owner_shape = jax.ShapeDtypeStruct((vocab_count, eight, width), bf16)
        target_shape = jax.ShapeDtypeStruct((eight, half), f32)
        first = turn == 0
        result = pl.pallas_call(
            functools.partial(owner_kernel, float(base_width * vocab_count), first),
            out_shape=(owner_shape, target_shape) if first else owner_shape,
            in_specs=[VMEM, VMEM],
            out_specs=(VMEM, VMEM) if first else VMEM,
            compiler_params=params,
            name="owner",
        )(got, target)
        if first:
            copies, target = result
        else:
            copies = result
        gaps = lax.all_to_all(copies, VOCAB, 0, 0, tiled=True).reshape(groups, 2, eight, width)
        kernel = functools.partial(step_kernel, last)
        operands = [gaps, active, base] + ([] if update is None else [update]) + [held]
        result = pl.pallas_call(
            no_update(kernel) if update is None else kernel,
            out_shape=update_shape if last else (update_shape, sent_shape),
            in_specs=[VMEM] * (len(operands) - 1) + [HBM],
            out_specs=VMEM if last else (VMEM, VMEM),
            scratch_shapes=[pltpu.VMEM((base_width, anchors), bf16), pltpu.VMEM((rows, anchors), bf16)]
            + ([] if last else [pltpu.VMEM((base_width, rows), f32), pltpu.VMEM((rows, anchors), f32)])
            + [pltpu.SemaphoreType.DMA((pieces,))],
            compiler_params=params,
            name="step",
        )(*operands)
        if last:
            update = result
        else:
            update, sent = result
    return update.T


def solution(mesh):
    split = Mesh(mesh.devices.reshape(mesh.shape["rows"], 4, 4, 2), ("rows",) + VOCAB)
    everywhere = ("rows",) + VOCAB
    in_specs = (
        P(None, everywhere),
        P(everywhere, None),
        P(),
        P("rows", VOCAB),
        P(VOCAB, None),
        P(),
        P("rows"),
    )
    return jax.shard_map(shards, mesh=split, in_specs=in_specs, out_specs=P("rows", VOCAB), check_vma=False)
```

profile of v0, /device:TPU:1, one launch (start us, length us, event | category | flops | bytes accessed | tf_op | source)
XLA Modules:
  0.0 197.6 jit_solution(10331620382053842781)
XLA Ops:
  0.0 0.7 broadcast_subtract_fusion
  0.7 0.0 copy-start.4
  0.7 1.2 copy-done.4
  1.9 0.0 copy-start.5
  1.9 0.9 copy-done.5
  2.9 2.1 %target_parts.1 = (f32[512,1024]{1,0:T(8,128)}, bf16[512,1024]{1,0:T(8,128)(2,1)S(1)}) custom-call(s32[1]{0:T(128)} %bitcast.2.core_ref, s32[1,2048]{1,0:T(1,128)S(1)} %bitcast.23, bf16[512,250]{1,0:T(8,128)(2,1)S(1)} %copy-done.5, bf16[250,2048]{1,0:T(8,128)(2,1)S(1)} %copy-done.4), custom_call_target="tpu_custom_call" | custom-call | tf_op jit(solution)/shard_map/target_parts/pallas_call | solution.py:222
  5.0 1.4 collective-permute-start
  6.4 0.7 select_convert_fusion
  7.1 0.0 copy-start
  7.1 1.6 copy-done
  8.7 12.6 %first_masses.1 = (bf16[4008,2048]{1,0:T(8,128)(2,1)}, bf16[16,2,8,1152]{3,2,1,0:T(8,128)(2,1)}) custom-call(s16[16,2048]{1,0:T(8,128)(2,1)S(1)} %broadcast_in_dim.17.tokens_ref, bf16[4008,2048]{1,0:T(8,128)(2,1)} %anchors_ref.2, f32[4008,128]{1,0:T(8,128)S(1)} %bitcast.16), custom_call_target="tpu_custom_call" | custom-call | tf_op jit(solution)/shard_map/first_masses/pallas_call | solution.py:238
  21.3 7.3 %all-to-all-start = ((bf16[32,8,1152]{2,1,0:T(8,128)(2,1)}), bf16[32,8,1152]{2,1,0:T(8,128)(2,1)S(1)}, u32[]{:S(2)}, u32[]{:S(2)}) async-start(bf16[32,8,1152]{2,1,0:T(8,128)(2,1)} %bitcast.1), calls=%async_computation | async-start | bytes 1179648 | tf_op jit(solution)/shard_map/all_to_all | solution.py:256
  28.6 0.0 collective-permute-done
  28.6 1.9 fusion
  30.6 0.0 copy-start.6
  30.6 10.3 %all-to-all-done.in_ref = bf16[32,8,1152]{2,1,0:T(8,128)(2,1)S(1)} async-done(((bf16[32,8,1152]{2,1,0:T(8,128)(2,1)}), bf16[32,8,1152]{2,1,0:T(8,128)(2,1)S(1)}, u32[]{:S(2)}, u32[]{:S(2)}) %all-to-all-start) | async-done | bytes 589856 | tf_op jit(solution)/shard_map/all_to_all | solution.py:256
  40.9 25.0 %all_to_all.35.target_ref = bf16[64,8,1024]{2,1,0:T(8,128)(2,1)S(1)} all-to-all(bf16[64,8,1024]{2,1,0:T(8,128)(2,1)S(1)} %fusion), channel_id=1, replica_groups=mesh['rows'=4,'x'=4,'y'=4,'core'=2] {'rows','x','y'}, dimensions={0} | all-to-all | bytes 2097152 | tf_op jit(solution)/shard_map/all_to_all | solution.py:233
  65.9 1.3 owner.3
  67.3 5.4 %all-to-all-start.2 = ((bf16[32,8,1152]{2,1,0:T(8,128)(2,1)}), bf16[32,8,1152]{2,1,0:T(8,128)(2,1)S(1)}, u32[]{:S(2)}, u32[]{:S(2)}) async-start(bf16[32,8,1152]{2,1,0:T(8,128)(2,1)} %get-tuple-element.18), calls=%async_computation.2 | async-start | bytes 1179648 | tf_op jit(solution)/shard_map/all_to_all | solution.py:272
  72.7 0.0 copy-done.6
  72.7 12.3 %all-to-all-done.2 = bf16[32,8,1152]{2,1,0:T(8,128)(2,1)S(1)} async-done(((bf16[32,8,1152]{2,1,0:T(8,128)(2,1)}), bf16[32,8,1152]{2,1,0:T(8,128)(2,1)S(1)}, u32[]{:S(2)}, u32[]{:S(2)}) %all-to-all-start.2) | async-done | bytes 589856 | tf_op jit(solution)/shard_map/all_to_all | solution.py:272
  85.0 15.7 %step.3 = (f32[4008,128]{1,0:T(8,128)S(1)}, bf16[16,2,8,1152]{3,2,1,0:T(8,128)(2,1)S(1)}) custom-call(bf16[16,2,8,1152]{3,2,1,0:T(8,128)(2,1)S(1)} %bitcast.20, f32[1,128]{1,0:T(1,128)S(1)} %convert_bitcast_fusion.active_ref, f32[4008,128]{1,0:T(8,128)} %bitcast.14, bf16[4008,2048]{1,0:T(8,128)(2,1)} %get-tuple-element.19.held_ref), custom_call_target="tpu_custom_call" | custom-call | tf_op jit(solution)/shard_map/step/pallas_call | solution.py:275
  100.7 0.0 copy-start.3
  100.7 1.3 copy-done.3
  102.0 15.7 %all_to_all.36.in_ref = bf16[32,8,1152]{2,1,0:T(8,128)(2,1)S(1)} all-to-all(bf16[32,8,1152]{2,1,0:T(8,128)(2,1)S(1)} %bitcast.22), channel_id=1, replica_groups=mesh['rows'=4,'x'=4,'y'=4,'core'=2] {'x','y','core'}, dimensions={0} | all-to-all | bytes 1179648 | tf_op jit(solution)/shard_map/all_to_all | solution.py:256
  117.7 0.4 owner.4
  118.0 15.7 %all_to_all.37 = bf16[32,8,1152]{2,1,0:T(8,128)(2,1)S(1)} all-to-all(bf16[32,8,1152]{2,1,0:T(8,128)(2,1)S(1)} %owner.4), channel_id=1, replica_groups=mesh['rows'=4,'x'=4,'y'=4,'core'=2] {'x','y','core'}, dimensions={0} | all-to-all | bytes 1179648 | tf_op jit(solution)/shard_map/all_to_all | solution.py:272
  133.7 16.3 %step.4 = (f32[4008,128]{1,0:T(8,128)S(1)}, bf16[16,2,8,1152]{3,2,1,0:T(8,128)(2,1)S(1)}) custom-call(bf16[16,2,8,1152]{3,2,1,0:T(8,128)(2,1)S(1)} %bitcast.18, f32[1,128]{1,0:T(1,128)S(1)} %convert_bitcast_fusion.active_ref, f32[4008,128]{1,0:T(8,128)} %bitcast.15, f32[4008,128]{1,0:T(8,128)} %copy-done.3, bf16[4008,2048]{1,0:T(8,128)(2,1)} %get-tuple-element.19.held_ref), custom_call_target="tpu_custom_call" | custom-call | tf_op jit(solution)/shard_map/step/pallas_call | solution.py:275
  150.1 0.0 copy-start.2
  150.1 1.3 copy-done.2
  151.4 0.0 copy-start.1
  151.4 15.8 %all_to_all.38.in_ref = bf16[32,8,1152]{2,1,0:T(8,128)(2,1)S(1)} all-to-all(bf16[32,8,1152]{2,1,0:T(8,128)(2,1)S(1)} %bitcast.21), channel_id=1, replica_groups=mesh['rows'=4,'x'=4,'y'=4,'core'=2] {'x','y','core'}, dimensions={0} | all-to-all | bytes 1179648 | tf_op jit(solution)/shard_map/all_to_all | solution.py:256
  167.2 0.4 owner.5
  167.6 15.7 %all_to_all.39 = bf16[32,8,1152]{2,1,0:T(8,128)(2,1)S(1)} all-to-all(bf16[32,8,1152]{2,1,0:T(8,128)(2,1)S(1)} %owner.5), channel_id=1, replica_groups=mesh['rows'=4,'x'=4,'y'=4,'core'=2] {'x','y','core'}, dimensions={0} | all-to-all | bytes 1179648 | tf_op jit(solution)/shard_map/all_to_all | solution.py:272
  183.3 0.0 copy-done.1
  183.3 14.1 %step.5 = f32[4008,128]{1,0:T(8,128)} custom-call(bf16[16,2,8,1152]{3,2,1,0:T(8,128)(2,1)S(1)} %bitcast.19, f32[1,128]{1,0:T(1,128)S(1)} %convert_bitcast_fusion.active_ref, f32[4008,128]{1,0:T(8,128)S(1)} %bitcast.17, f32[4008,128]{1,0:T(8,128)} %copy-done.2, bf16[4008,2048]{1,0:T(8,128)(2,1)} %get-tuple-element.19.held_ref), custom_call_target="tpu_custom_call" | custom-call | tf_op jit(solution)/shard_map/step/pallas_call | solution.py:275
  (2 shorter events, 0.0 us)
Async XLA Ops:
  0.7 1.2 copy-start.4
  1.9 0.9 copy-start.5
  5.0 23.6 %collective-permute-start = (bf16[512,1024]{1,0:T(8,128)(2,1)S(1)}, bf16[512,1024]{1,0:T(8,128)(2,1)S(1)}, u32[]{:S(2)}, u32[]{:S(2)}) collective-permute-start(bf16[512,1024]{1,0:T(8,128)(2,1)S(1)} %get-tuple-element.17), channel_id=1, source_target_pairs={{0,1},{1,0},{2,3},{3,2},{4,5},{5,4},{6,7},{7,6},{8,9},{9,8},{10,11... | collective-permute-start | bytes 3145736 | tf_op jit(solution)/shard_map/ppermute | solution.py:230
  7.1 1.6 copy-start
  21.3 19.6 %all-to-all-start = ((bf16[32,8,1152]{2,1,0:T(8,128)(2,1)}), bf16[32,8,1152]{2,1,0:T(8,128)(2,1)S(1)}, u32[]{:S(2)}, u32[]{:S(2)}) async-start(bf16[32,8,1152]{2,1,0:T(8,128)(2,1)} %bitcast.1), calls=%async_computation | async-start | bytes 1179648 | tf_op jit(solution)/shard_map/all_to_all | solution.py:256
  30.6 42.1 %copy-start.6 = (s32[128]{0:T(128)S(1)}, s32[128]{0:T(128)}, u32[]{:S(2)}) copy-start(s32[128]{0:T(128)} %param.13) | copy-start | bytes 1540
  67.3 17.7 %all-to-all-start.2 = ((bf16[32,8,1152]{2,1,0:T(8,128)(2,1)}), bf16[32,8,1152]{2,1,0:T(8,128)(2,1)S(1)}, u32[]{:S(2)}, u32[]{:S(2)}) async-start(bf16[32,8,1152]{2,1,0:T(8,128)(2,1)} %get-tuple-element.18), calls=%async_computation.2 | async-start | bytes 1179648 | tf_op jit(solution)/shard_map/all_to_all | solution.py:272
  100.7 1.3 copy-start.3
  150.1 1.3 copy-start.2
  151.4 31.9 %copy-start.1 = (f32[128,4008]{0,1:T(8,128)S(1)}, f32[128,4008]{0,1:T(8,128)}, u32[]{:S(2)}) copy-start(f32[128,4008]{0,1:T(8,128)} %param.10) | copy-start | bytes 6156292
where the time goes:
time: 198 us
  blocking collectives  88 us (44%)
  Pallas kernels  62.9 us (32%)
  waiting for transfers between devices  22.6 us (11%)
  starting transfers between devices  14.1 us (7%)
  local copies, waits for them, and re-layouts  6.36 us (3%)
  other arithmetic  3.34 us (2%)
    pallas_call x3, Pallas kernels, shards(): pl.pallas_call(no_update(kernel) if update is None else kernel, out_shape...  46.1 us
    all_to_all x2, blocking collectives, shards(): lax.all_to_all(sent.reshape(vocab_count, eight, width), VOCAB, 0, 0, tile...  31.5 us
    all_to_all x2, blocking collectives, shards(): lax.all_to_all(copies, VOCAB, 0, 0, tiled=True)  31.4 us
    all_to_all x1, blocking collectives, shards(): target = lax.all_to_all(target, CHIPS, 0, 0, tiled=True)  25 us
    pallas_call x1, Pallas kernels, shards(): pl.pallas_call(first_kernel, out_shape=(held_shape, sent_shape), in_specs...  12.6 us
    all_to_all x1, waiting for transfers between devices, shards(): lax.all_to_all(copies, VOCAB, 0, 0, tiled=True)  12.3 us
    all_to_all x1, waiting for transfers between devices, shards(): lax.all_to_all(sent.reshape(vocab_count, eight, width), VOCAB, 0, 0, tile...  10.3 us
    all_to_all x1, starting transfers between devices, shards(): lax.all_to_all(sent.reshape(vocab_count, eight, width), VOCAB, 0, 0, tile...  7.32 us
  transfers between devices with their start and end apart: 3, of which 2 were waited for; matrix products, arithmetic and copies ran while one was open for 1% of the time, Pallas kernels for 6%

commit v1 on v0

v1 whole, which is shorter than its diff:
```python
import functools
import jax
import jax.numpy as jnp
from jax import lax
from jax.experimental import pallas as pl
from jax.experimental.pallas import tpu as pltpu
from jax.sharding import Mesh
from jax.sharding import PartitionSpec as P

ITERATIONS = 3
VOCAB = ("x", "y", "core")
CHIPS = ("rows", "x", "y")
LANES = 128
CHUNK = 512
AHEAD = 2
epsilon = 1e-06
step_size = 2.0

def grant(mebibytes):
    return pltpu.CompilerParams(vmem_limit_bytes=mebibytes * 1024 * 1024)


HBM = pl.BlockSpec(memory_space=pl.ANY)
VMEM = pl.BlockSpec(memory_space=pltpu.VMEM)
SMEM = pl.BlockSpec(memory_space=pltpu.SMEM)


def chunks_of(extent):
    starts = list(range(0, extent, CHUNK))
    return [(start, min(CHUNK, extent - start)) for start in starts]


def three_parts(value):
    high = value.astype(jnp.bfloat16).astype(jnp.float32)
    rest = value - high
    middle = rest.astype(jnp.bfloat16).astype(jnp.float32)
    return high, middle, rest - middle


def matmul_nt(left, right):
    return lax.dot_general(left, right, (((1,), (1,)), ((), ())), preferred_element_type=jnp.float32)


def with_self(block, tokens, start):
    rows, columns = block.shape
    if rows % 16 == 0:
        place = lax.broadcasted_iota(jnp.int16, (rows, columns), 0) + jnp.int16(start)
        wanted = jnp.broadcast_to(tokens[None], (rows // 16, 16, columns)).reshape(rows, columns)
    else:
        place = lax.broadcasted_iota(jnp.int16, (rows, columns), 0) + jnp.int16(start)
        whole = -(-rows // 16)
        wanted = jnp.broadcast_to(tokens[None], (whole, 16, columns)).reshape(whole * 16, columns)[:rows]
    return jnp.where(place == wanted, block + jnp.bfloat16(1), block)


def put_masses(core, logits_ref, anchors_of, mine_ref, other_ref, mass_ref):
    extent, rows = logits_ref.shape
    top = jnp.max(logits_ref[...], axis=0, keepdims=True)
    total = jnp.zeros((1, rows), jnp.float32)
    for start, size in chunks_of(extent):
        weights = jnp.exp(logits_ref[pl.ds(start, size), :] - top)
        total = total + jnp.sum(weights, axis=0, keepdims=True)
        turned = weights.T.astype(jnp.bfloat16)
        part = jnp.dot(turned, anchors_of(start, size), preferred_element_type=jnp.float32)
        if start == 0:
            mass_ref[...] = part
        else:
            mass_ref[...] += part
    groups, eight, width = mine_ref.shape
    half = width - LANES
    parts = three_parts(top) + three_parts(total)
    stats = jnp.concatenate(list(parts) + [jnp.zeros((LANES - len(parts), rows), jnp.float32)], axis=0)
    stats = stats.T.reshape(groups, eight, LANES).astype(jnp.bfloat16)
    for out_ref, which in ((mine_ref, core), (other_ref, 1 - core)):
        columns = pl.ds(pl.multiple_of(which * half, half), half)
        out_ref[:, :, :half] = mass_ref[:, columns].reshape(groups, eight, half).astype(jnp.bfloat16)
        out_ref[:, :, half:] = stats


def first_kernel(place_ref, tokens_ref, anchors_ref, logits_hbm, held_ref, mine_ref, other_ref, buffer, logits_ref, mass_ref, sem_in, sem_out, sem_base):
    extent, rows = logits_ref.shape
    base = pltpu.make_async_copy(logits_hbm, logits_ref, sem_base)
    base.start()
    loads, stores = [], []
    for i, (start, size) in enumerate(chunks_of(extent)):
        where = pl.ds(start, size)
        loads.append(pltpu.make_async_copy(anchors_ref.at[where], buffer.at[where], sem_in.at[i]))
    for load in loads[:AHEAD]:
        load.start()
    shifted = tokens_ref[...] - place_ref[0]
    shifted = jnp.where((shifted >= 0) & (shifted < extent), shifted, -1)
    tokens = jnp.broadcast_to(shifted, (16, shifted.shape[1])).astype(jnp.int16)
    base.wait()

    def anchors_of(start, size):
        i = start // CHUNK
        where = pl.ds(start, size)
        loads[i].wait()
        if i + AHEAD < len(loads):
            loads[i + AHEAD].start()
        buffer[where, :] = with_self(buffer[where, :], tokens, start)
        store = pltpu.make_async_copy(buffer.at[where], held_ref.at[where], sem_out.at[i])
        store.start()
        stores.append(store)
        return buffer[where, :]

    put_masses(place_ref[1], logits_ref, anchors_of, mine_ref, other_ref, mass_ref)
    for store in stores:
        store.wait()


def lane_sum(stats, which):
    lane = lax.broadcasted_iota(jnp.int32, stats.shape, stats.ndim - 1)
    chosen = (lane >= 3 * which) & (lane < 3 * which + 3)
    return jnp.sum(jnp.where(chosen, stats, 0.0), axis=-1, keepdims=True)


def lane_tile(shape, values):
    lane = lax.broadcasted_iota(jnp.int32, shape, len(shape) - 1)
    tile = jnp.zeros(shape, jnp.float32)
    for i, part in enumerate(part for value in values for part in three_parts(value)):
        tile = jnp.where(lane == i, part, tile)
    return tile.astype(jnp.bfloat16)


def pair_kernel(mine_ref, other_ref, out_ref):
    half = out_ref.shape[2] - LANES
    stats = [ref[:, :, half:].astype(jnp.float32) for ref in (mine_ref, other_ref)]
    tops = [lane_sum(stat, 0) for stat in stats]
    top = jnp.maximum(*tops)
    factors = [jnp.exp(each - top) for each in tops]
    total = sum(lane_sum(stat, 1) * factor for stat, factor in zip(stats, factors))
    mine = mine_ref[:, :, :half].astype(jnp.float32) * factors[0]
    other = other_ref[:, :, :half].astype(jnp.float32) * factors[1]
    out_ref[:, :, :half] = (mine + other).astype(jnp.bfloat16)
    out_ref[:, :, half:] = lane_tile(stats[0].shape, (top, total))


def owner_kernel(full_vocab, first, in_ref, target_ref, out_ref, sum_ref=None):
    half = in_ref.shape[2] - LANES
    if first:
        target = jnp.sum(target_ref[...].astype(jnp.float32), axis=0)
        sum_ref[...] = target
    else:
        target = target_ref[...]
    stats = in_ref[:, :, half:].astype(jnp.float32)
    top = lane_sum(stats, 0)
    row_max = jnp.max(top, axis=0, keepdims=True)
    factor = jnp.exp(top - row_max)
    total = jnp.sum(lane_sum(stats, 1) * factor, axis=0)
    mass = jnp.sum(in_ref[:, :, :half].astype(jnp.float32) * factor, axis=0)
    gap = full_vocab * mass / total - target
    sent = gap.astype(jnp.bfloat16)
    squares = jnp.sum(gap * gap, axis=1, keepdims=True)
    inner = jnp.sum(sent.astype(jnp.float32) * mass, axis=1, keepdims=True)
    tile = lane_tile((in_ref.shape[1], LANES), (row_max[0], total, squares, inner))
    out_ref[:, :, :half] = jnp.broadcast_to(sent[None], (in_ref.shape[0],) + sent.shape)
    out_ref[:, :, half:] = jnp.broadcast_to(tile[None], (in_ref.shape[0],) + tile.shape)


def step_kernel(last, place_ref, mine_gap_ref, other_gap_ref, active_ref, base_ref, update_ref, held_ref, *rest):
    if last:
        new_ref, gap_all = rest
    else:
        new_ref, mine_ref, other_ref, gap_all, logits_ref, mass_ref = rest
    extent, rows = base_ref.shape
    half = mine_gap_ref.shape[2] - LANES
    core = place_ref[1]
    stats = []
    for gap_ref, which in ((mine_gap_ref, core), (other_gap_ref, 1 - core)):
        columns = pl.ds(pl.multiple_of(which * half, half), half)
        piece = gap_ref[:, :, :half].astype(jnp.float32).reshape(rows, half)
        gap_all[:, columns] = piece.astype(jnp.bfloat16)
        stats.append(gap_ref[:, :, half:].astype(jnp.float32).reshape(rows, LANES).T)

    def joined(which, h):
        return jnp.sum(stats[h][3 * which : 3 * which + 3], axis=0, keepdims=True)

    row_max, total = joined(0, 0), joined(1, 0)
    squares = joined(2, 0) + joined(2, 1)
    inner = joined(3, 0) + joined(3, 1)
    scale = lax.rsqrt(squares / (2 * half) + epsilon)
    slope = scale * inner / total
    active = active_ref[...].astype(jnp.float32)
    for start, size in chunks_of(extent):
        where = pl.ds(start, size)
        back = matmul_nt(held_ref[where, :], gap_all[...]) * scale
        logits = base_ref[where, :]
        if update_ref is not None:
            logits = logits + update_ref[where, :]
        weights = jnp.exp(logits - row_max)
        change = -step_size * active * weights * (back - slope)
        new_ref[where, :] = change if update_ref is None else update_ref[where, :] + change
        if not last:
            logits_ref[where, :] = logits + change
    if not last:
        put_masses(core, logits_ref, lambda start, size: held_ref[pl.ds(start, size), :], mine_ref, other_ref, mass_ref)


def no_update(kernel):
    def run(place_ref, mine_gap_ref, other_gap_ref, active_ref, base_ref, held_ref, *rest):
        kernel(place_ref, mine_gap_ref, other_gap_ref, active_ref, base_ref, None, held_ref, *rest)

    return run


def target_kernel(place_ref, tokens_ref, *rest):
    out_ref = rest[-1]
    half = out_ref.shape[1]
    columns = pl.ds(pl.multiple_of(place_ref[0] * half, half), half)
    tokens = tokens_ref[:, columns]
    total = None
    for i in range(2):
        delta_ref, anchors_ref = rest[2 * i : 2 * i + 2]
        block = anchors_ref[:, columns].astype(jnp.float32)
        place = lax.broadcasted_iota(jnp.int32, block.shape, 0) + place_ref[1 + i]
        block = jnp.where(place == tokens, block + 1.0, block).astype(jnp.bfloat16)
        part = jnp.dot(delta_ref[...], block, preferred_element_type=jnp.float32)
        total = part if total is None else total + part
    out_ref[...] = total.astype(jnp.bfloat16)


def shards(expert_delta, small_anchors, small_tokens, base_logits, base_anchors, base_tokens, active_rows):
    f32, bf16 = jnp.float32, jnp.bfloat16
    vocab_count = lax.axis_size(VOCAB)
    vocab_place = lax.axis_index(VOCAB)
    place = lax.axis_index("rows") * vocab_count + vocab_place
    all_rows, small_width = expert_delta.shape
    base_width, anchors = base_anchors.shape
    rows = base_logits.shape[0]
    half = anchors // 2
    width = half + LANES
    eight = 2 * rows // vocab_count
    groups = vocab_count // 2
    pieces = len(chunks_of(base_width))

    core = lax.axis_index("core")
    small_place = jnp.stack([core, place * small_width, (place + 1 - 2 * core) * small_width])
    base_place = jnp.stack([vocab_place * base_width, core])
    small_tokens, base_tokens = small_tokens[None, :], base_tokens[None, :]
    active = active_rows[None, :]
    base = base_logits.T

    swap = [(0, 1), (1, 0)]
    other_delta = lax.ppermute(expert_delta, "core", swap)
    other_anchors = lax.ppermute(small_anchors, "core", swap)
    target = pl.pallas_call(
        target_kernel,
        out_shape=jax.ShapeDtypeStruct((all_rows, half), bf16),
        in_specs=[SMEM, VMEM, VMEM, VMEM, VMEM, VMEM],
        out_specs=VMEM,
        compiler_params=grant(16),
        name="target_parts",
    )(small_place, small_tokens, expert_delta, small_anchors, other_delta, other_anchors)
    target = lax.all_to_all(target.reshape(-1, eight, half), CHIPS, 0, 0, tiled=True)

    sent_shape = jax.ShapeDtypeStruct((groups, eight, width), bf16)
    held_shape = jax.ShapeDtypeStruct((base_width, anchors), bf16)
    update_shape = jax.ShapeDtypeStruct((base_width, rows), f32)
    held, mine, other = pl.pallas_call(
        first_kernel,
        out_shape=(held_shape, sent_shape, sent_shape),
        in_specs=[SMEM, VMEM, HBM, HBM],
        out_specs=(HBM, VMEM, VMEM),
        scratch_shapes=[
            pltpu.VMEM((base_width, anchors), bf16),
            pltpu.VMEM((base_width, rows), f32),
            pltpu.VMEM((rows, anchors), f32),
            pltpu.SemaphoreType.DMA((pieces,)),
            pltpu.SemaphoreType.DMA((pieces,)),
            pltpu.SemaphoreType.DMA,
        ],
        compiler_params=grant(36),
        name="first_masses",
    )(base_place, base_tokens, base_anchors, base)

    def both(mine, other):
        other = lax.ppermute(other, "core", swap)
        return pl.pallas_call(
            pair_kernel,
            out_shape=sent_shape,
            in_specs=[VMEM, VMEM],
            out_specs=VMEM,
            compiler_params=grant(4),
            name="pair",
        )(mine, other)

    sent, target = lax.optimization_barrier((both(mine, other), target))
    update = None
    for turn in range(ITERATIONS):
        last = turn == ITERATIONS - 1
        got = lax.all_to_all(sent, CHIPS[1:], 0, 0, tiled=True)
        target_shape = jax.ShapeDtypeStruct((eight, half), f32)
        first = turn == 0
        result = pl.pallas_call(
            functools.partial(owner_kernel, float(base_width * vocab_count), first),
            out_shape=(sent_shape, target_shape) if first else sent_shape,
            in_specs=[VMEM, VMEM],
            out_specs=(VMEM, VMEM) if first else VMEM,
            compiler_params=grant(4),
            cost_estimate=pl.CostEstimate(flops=20_000_000_000, bytes_accessed=40_000_000, transcendentals=0) if first else None,
            name="owner",
        )(got, target)
        if first:
            copies, target = result
        else:
            copies = result
        gaps = lax.all_to_all(copies, CHIPS[1:], 0, 0, tiled=True)
        other_gaps = lax.ppermute(gaps, "core", swap)
        kernel = functools.partial(step_kernel, last)
        operands = [base_place, gaps, other_gaps, active, base] + ([] if update is None else [update]) + [held]
        result = pl.pallas_call(
            no_update(kernel) if update is None else kernel,
            out_shape=update_shape if last else (update_shape, sent_shape, sent_shape),
            in_specs=[SMEM] + [VMEM] * (len(operands) - 1),
            out_specs=VMEM if last else (VMEM, VMEM, VMEM),
            scratch_shapes=[pltpu.VMEM((rows, anchors), bf16)]
            + ([] if last else [pltpu.VMEM((base_width, rows), f32), pltpu.VMEM((rows, anchors), f32)]),
            compiler_params=grant(16),
            name="step",
        )(*operands)
        if last:
            update = result
        else:
            update, mine, other = result
            sent = both(mine, other)
    return update.T


def solution(mesh):
    split = Mesh(mesh.devices.reshape(mesh.shape["rows"], 4, 4, 2), ("rows",) + VOCAB)
    everywhere = ("rows",) + VOCAB
    in_specs = (
        P(None, everywhere),
        P(everywhere, None),
        P(),
        P("rows", VOCAB),
        P(VOCAB, None),
        P(),
        P("rows"),
    )
    return jax.shard_map(shards, mesh=split, in_specs=in_specs, out_specs=P("rows", VOCAB), check_vma=False)
```

time: 198 us -> 149 us (0.75)
  Pallas kernels: 62.9 us -> 41.8 us
  blocking collectives: 88 us -> 68.2 us
  waiting for transfers between devices: 22.6 us -> 12.1 us
  starting transfers between devices: 14.1 us -> 23.1 us
  local copies, waits for them, and re-layouts: 6.36 us -> 2.9 us
  other arithmetic: 3.34 us -> 0.15 us
    pallas_call x3, Pallas kernels: 46.1 us -> 24.4 us  [shards(): pl.pallas_call(no_update(kernel) if update is None else kernel, out_shape...]
    all_to_all x2 -> x1, waiting for transfers between devices: 22.6 us -> 2.01 us  [shards(): lax.all_to_all(target.reshape(-1, eight, half), CHIPS, 0, 0, tiled=True)]
    all_to_all x5 -> x6, blocking collectives: 88 us -> 68.2 us  [the longest x3 34.2 us: shards(): got = lax.all_to_all(sent, CHIPS[1:], 0, 0, tiled=True)]
    ppermute x1 -> x8, starting transfers between devices: 1.38 us -> 11.8 us  [the longest x3 8.83 us: shards(): other_gaps = lax.ppermute(gaps, 'core', swap)]
    ppermute x1 -> x8, waiting for transfers between devices: 0.01 us -> 10.1 us  [the longest x3 3.63 us: both(): other = lax.ppermute(other, 'core', swap)]
    unnamed x14 -> x20, local copies, waits for them, and re-layouts: 6.35 us -> 2.9 us
    pallas_call x2 -> x5, Pallas kernels: 14.8 us -> 16.5 us  [the longest x1 13.4 us: shards(): pl.pallas_call(first_kernel, out_shape=(held_shape, sent_shape, sent_shap...]
    all_to_all x2 -> x1, starting transfers between devices: 12.7 us -> 11.2 us  [shards(): lax.all_to_all(target.reshape(-1, eight, half), CHIPS, 0, 0, tiled=True)]
  transfers between devices with their start and end apart: 3 -> 9, of which waited for: 2 -> 8; matrix products, arithmetic and copies ran while one was open for 1% -> 0% of each run, Pallas kernels for 6% -> 9%
where the time goes in v1:
time: 149 us; the launch traced here: 148 us
  blocking collectives  68.2 us (46%)
  Pallas kernels  41.8 us (28%)
  starting transfers between devices  23.1 us (16%)
  waiting for transfers between devices  12.1 us (8%)
  local copies, waits for them, and re-layouts  2.9 us (2%)
    all_to_all x3, blocking collectives, shards(): got = lax.all_to_all(sent, CHIPS[1:], 0, 0, tiled=True)  34.2 us
    all_to_all x3, blocking collectives, shards(): gaps = lax.all_to_all(copies, CHIPS[1:], 0, 0, tiled=True)  33.9 us
    pallas_call x3, Pallas kernels, shards(): pl.pallas_call(no_update(kernel) if update is None else kernel, out_shape...  24.4 us
    pallas_call x1, Pallas kernels, shards(): pl.pallas_call(first_kernel, out_shape=(held_shape, sent_shape, sent_shap...  13.4 us
    all_to_all x1, starting transfers between devices, shards(): lax.all_to_all(target.reshape(-1, eight, half), CHIPS, 0, 0, tiled=True)  11.2 us
    ppermute x3, starting transfers between devices, shards(): other_gaps = lax.ppermute(gaps, 'core', swap)  8.83 us
    ppermute x3, waiting for transfers between devices, both(): other = lax.ppermute(other, 'core', swap)  3.63 us
    ppermute x3, waiting for transfers between devices, shards(): other_gaps = lax.ppermute(gaps, 'core', swap)  3.63 us
  transfers between devices with their start and end apart: 9, of which 8 were waited for; matrix products, arithmetic and copies ran while one was open for 0% of the time, Pallas kernels for 9%

profile of v1, /device:TPU:1, one launch (start us, length us, event | category | flops | bytes accessed | tf_op | source)
XLA Modules:
  0.0 148.2 jit_solution(1823072487907069119)
XLA Ops:
  0.0 1.4 collective-permute-start.2
  1.4 0.0 collective-permute-start.1
  1.4 0.1 pad_add_fusion.1.place_ref
  1.5 2.8 %collective-permute-done.1.rest_2_ = bf16[512,250]{1,0:T(8,128)(2,1)S(1)} collective-permute-done((bf16[512,250]{1,0:T(8,128)(2,1)}, bf16[512,250]{1,0:T(8,128)(2,1)S(1)}, u32[]{:S(2)}, u32[]{:S(2)}) %collective-permute-start.1) | collective-permute-done | bytes 256032 | tf_op jit(solution)/shard_map/ppermute | solution.py:245
  4.3 0.0 collective-permute-done.2.rest_3_
  4.3 0.0 copy-start.1
  4.3 1.2 copy-done.1
  5.5 0.0 copy-start.2
  5.5 0.9 copy-done.2
  6.4 0.0 copy-start.3
  6.4 0.7 copy-done.3
  7.1 0.0 copy-start
  7.1 0.0 copy-start.4
  7.1 2.3 %target_parts.1 = bf16[512,1024]{1,0:T(8,128)(2,1)} custom-call(s32[3]{0:T(128)S(1)} %pad_add_fusion.1.place_ref, s32[1,2048]{1,0:T(1,128)S(1)} %bitcast.16, bf16[512,250]{1,0:T(8,128)(2,1)S(1)} %copy-done.2, bf16[250,2048]{1,0:T(8,128)(2,1)S(1)} %copy-done.1, bf16[512,250]{1,0:T(8,128)(2,1)S(1)} %collective-permute-done.1.rest_2_, ...), custom_call_target="tpu_custom_call" | custom-call | tf_op jit(solution)/shard_map/target_parts/pallas_call | solution.py:247
  9.4 11.2 %all-to-all-start = ((bf16[64,8,1024]{2,1,0:T(8,128)(2,1)}), bf16[64,8,1024]{2,1,0:T(8,128)(2,1)S(1)}, u32[]{:S(2)}, u32[]{:S(2)}) async-start(bf16[64,8,1024]{2,1,0:T(8,128)(2,1)} %bitcast.7), calls=%async_computation | async-start | bytes 2097152 | tf_op jit(solution)/shard_map/all_to_all | solution.py:255
  20.7 0.1 pad_add_fusion.place_ref
  20.8 0.0 copy-done
  20.8 0.0 copy-done.4
  20.8 13.4 %first_masses.1 = (bf16[4008,2048]{1,0:T(8,128)(2,1)}, bf16[16,8,1152]{2,1,0:T(8,128)(2,1)S(1)}, bf16[16,8,1152]{2,1,0:T(8,128)(2,1)S(1)}) custom-call(s32[2]{0:T(128)S(1)} %pad_add_fusion.place_ref, s32[1,2048]{1,0:T(1,128)S(1)} %bitcast.17, bf16[4008,2048]{1,0:T(8,128)(2,1)} %anchors_ref.1, f32[4008,128]{1,0:T(8,128)S(1)} %bitcast.12), custom_call_target="tpu_custom_call" | custom-call | tf_op jit(solution)/shard_map/first_masses/pallas_call | solution.py:260
  34.2 0.7 collective-permute-start
  34.9 1.2 collective-permute-done.other_ref
  36.1 0.3 pair.3
  36.4 2.0 %all-to-all-done.target_ref = bf16[64,8,1024]{2,1,0:T(8,128)(2,1)S(1)} async-done(((bf16[64,8,1024]{2,1,0:T(8,128)(2,1)}), bf16[64,8,1024]{2,1,0:T(8,128)(2,1)S(1)}, u32[]{:S(2)}, u32[]{:S(2)}) %all-to-all-start) | async-done | bytes 1048608 | tf_op jit(solution)/shard_map/all_to_all | solution.py:255
  38.4 0.0 slice-start
  38.4 12.4 %all_to_all.35.in_ref = bf16[16,8,1152]{2,1,0:T(8,128)(2,1)S(1)} all-to-all(bf16[16,8,1152]{2,1,0:T(8,128)(2,1)S(1)} %pair.3), channel_id=1, replica_groups=mesh['rows'=4,'x'=4,'y'=4,'core'=2] {'x','y'}, dimensions={0} | all-to-all | bytes 589824 | tf_op jit(solution)/shard_map/all_to_all | solution.py:292
  50.8 0.0 slice-start.1
  50.8 0.0 slice-start.2
  50.8 0.0 slice-start.3
  50.8 0.0 copy-start.5
  50.8 0.4 owner.3
  51.2 11.5 %all_to_all.36.mine_gap_ref = bf16[16,8,1152]{2,1,0:T(8,128)(2,1)S(1)} all-to-all(bf16[16,8,1152]{2,1,0:T(8,128)(2,1)S(1)} %get-tuple-element.22), channel_id=1, replica_groups=mesh['rows'=4,'x'=4,'y'=4,'core'=2] {'x','y'}, dimensions={0} | all-to-all | bytes 589824 | tf_op jit(solution)/shard_map/all_to_all | solution.py:308
  62.7 2.9 %collective-permute-start.3 = (bf16[16,8,1152]{2,1,0:T(8,128)(2,1)S(1)}, bf16[16,8,1152]{2,1,0:T(8,128)(2,1)S(1)}, u32[]{:S(2)}, u32[]{:S(2)}) collective-permute-start(bf16[16,8,1152]{2,1,0:T(8,128)(2,1)S(1)} %all_to_all.36.mine_gap_ref), channel_id=1, source_target_pairs={{0,1},{1,0},{2,3},{3,2},{4,5},{5,4},{6,7},{7,6},{8,9},{9,8},{10,11... | collective-permute-start | bytes 884744 | tf_op jit(solution)/shard_map/ppermute | solution.py:309
  65.6 1.2 collective-permute-done.3.other_gap_ref
  66.8 0.0 slice-done
  66.8 0.0 slice-done.1
  66.8 0.0 slice-done.2
  66.8 0.0 slice-done.3
  66.8 0.0 copy-done.5
  66.9 9.0 %step.3 = (f32[4008,128]{1,0:T(8,128)S(1)}, bf16[16,8,1152]{2,1,0:T(8,128)(2,1)S(1)}, bf16[16,8,1152]{2,1,0:T(8,128)(2,1)S(1)}) custom-call(s32[2]{0:T(128)S(1)} %pad_add_fusion.place_ref, bf16[16,8,1152]{2,1,0:T(8,128)(2,1)S(1)} %all_to_all.36.mine_gap_ref, bf16[16,8,1152]{2,1,0:T(8,128)(2,1)S(1)} %collective-permute-done.3.other_gap_ref, ...), custom_call_target="tpu_custom_call" | custom-call | tf_op jit(solution)/shard_map/step/pallas_call | solution.py:312
  75.8 0.5 collective-permute-start.4
  76.3 1.2 collective-permute-done.4.other_ref
  77.5 0.3 pair.4
  77.8 10.9 %all_to_all.37.in_ref = bf16[16,8,1152]{2,1,0:T(8,128)(2,1)S(1)} all-to-all(bf16[16,8,1152]{2,1,0:T(8,128)(2,1)S(1)} %pair.4), channel_id=1, replica_groups=mesh['rows'=4,'x'=4,'y'=4,'core'=2] {'x','y'}, dimensions={0} | all-to-all | bytes 589824 | tf_op jit(solution)/shard_map/all_to_all | solution.py:292
  88.7 0.3 owner.4
  89.0 11.2 %all_to_all.38.mine_gap_ref = bf16[16,8,1152]{2,1,0:T(8,128)(2,1)S(1)} all-to-all(bf16[16,8,1152]{2,1,0:T(8,128)(2,1)S(1)} %owner.4), channel_id=1, replica_groups=mesh['rows'=4,'x'=4,'y'=4,'core'=2] {'x','y'}, dimensions={0} | all-to-all | bytes 589824 | tf_op jit(solution)/shard_map/all_to_all | solution.py:308
  100.2 2.9 %collective-permute-start.5 = (bf16[16,8,1152]{2,1,0:T(8,128)(2,1)S(1)}, bf16[16,8,1152]{2,1,0:T(8,128)(2,1)S(1)}, u32[]{:S(2)}, u32[]{:S(2)}) collective-permute-start(bf16[16,8,1152]{2,1,0:T(8,128)(2,1)S(1)} %all_to_all.38.mine_gap_ref), channel_id=1, source_target_pairs={{0,1},{1,0},{2,3},{3,2},{4,5},{5,4},{6,7},{7,6},{8,9},{9,8},{10,11... | collective-permute-start | bytes 884744 | tf_op jit(solution)/shard_map/ppermute | solution.py:309
  103.1 1.2 collective-permute-done.5.other_gap_ref
  104.3 9.0 %step.4 = (f32[4008,128]{1,0:T(8,128)S(1)}, bf16[16,8,1152]{2,1,0:T(8,128)(2,1)S(1)}, bf16[16,8,1152]{2,1,0:T(8,128)(2,1)S(1)}) custom-call(s32[2]{0:T(128)S(1)} %pad_add_fusion.place_ref, bf16[16,8,1152]{2,1,0:T(8,128)(2,1)S(1)} %all_to_all.38.mine_gap_ref, bf16[16,8,1152]{2,1,0:T(8,128)(2,1)S(1)} %collective-permute-done.5.other_gap_ref, ...), custom_call_target="tpu_custom_call" | custom-call | tf_op jit(solution)/shard_map/step/pallas_call | solution.py:312
  113.4 0.5 collective-permute-start.6
  113.8 1.2 collective-permute-done.6.other_ref
  115.0 0.3 pair.5
  115.3 10.9 %all_to_all.39.in_ref = bf16[16,8,1152]{2,1,0:T(8,128)(2,1)S(1)} all-to-all(bf16[16,8,1152]{2,1,0:T(8,128)(2,1)S(1)} %pair.5), channel_id=1, replica_groups=mesh['rows'=4,'x'=4,'y'=4,'core'=2] {'x','y'}, dimensions={0} | all-to-all | bytes 589824 | tf_op jit(solution)/shard_map/all_to_all | solution.py:292
  126.2 0.3 owner.5
  126.5 11.2 %all_to_all.40.mine_gap_ref = bf16[16,8,1152]{2,1,0:T(8,128)(2,1)S(1)} all-to-all(bf16[16,8,1152]{2,1,0:T(8,128)(2,1)S(1)} %owner.5), channel_id=1, replica_groups=mesh['rows'=4,'x'=4,'y'=4,'core'=2] {'x','y'}, dimensions={0} | all-to-all | bytes 589824 | tf_op jit(solution)/shard_map/all_to_all | solution.py:308
  137.7 2.9 %collective-permute-start.7 = (bf16[16,8,1152]{2,1,0:T(8,128)(2,1)S(1)}, bf16[16,8,1152]{2,1,0:T(8,128)(2,1)S(1)}, u32[]{:S(2)}, u32[]{:S(2)}) collective-permute-start(bf16[16,8,1152]{2,1,0:T(8,128)(2,1)S(1)} %all_to_all.40.mine_gap_ref), channel_id=1, source_target_pairs={{0,1},{1,0},{2,3},{3,2},{4,5},{5,4},{6,7},{7,6},{8,9},{9,8},{10,11... | collective-permute-start | bytes 884744 | tf_op jit(solution)/shard_map/ppermute | solution.py:309
  140.6 1.2 collective-permute-done.7.other_gap_ref
  141.8 6.4 %step.5 = f32[4008,128]{1,0:T(8,128)} custom-call(s32[2]{0:T(128)S(1)} %pad_add_fusion.place_ref, bf16[16,8,1152]{2,1,0:T(8,128)(2,1)S(1)} %all_to_all.40.mine_gap_ref, bf16[16,8,1152]{2,1,0:T(8,128)(2,1)S(1)} %collective-permute-done.7.other_gap_ref, s32[1,128]{1,0:T(1,128)S(1)} %bitcast.20, f32[4008,128]{1,0:T(8,128)S(1)} %bitcast.15, ...), custom_call_target="tpu_custom_call" | custom-call | tf_op jit(solution)/shard_map/step/pallas_call | solution.py:312
  (1 shorter events, 0.0 us)
Async XLA Ops:
  0.0 4.3 %collective-permute-start.2 = (bf16[250,2048]{1,0:T(8,128)(2,1)}, bf16[250,2048]{1,0:T(8,128)(2,1)S(1)}, u32[]{:S(2)}, u32[]{:S(2)}) collective-permute-start(bf16[250,2048]{1,0:T(8,128)(2,1)} %rest_1_.1), channel_id=1, source_target_pairs={{0,1},{1,0},{2,3},{3,2},{4,5},{5,4},{6,7},{7,6},{8,9},{9,8},{10,11... | collective-permute-start | bytes 3072008 | tf_op jit(solution)/shard_map/ppermute | solution.py:246
  1.4 2.9 %collective-permute-start.1 = (bf16[512,250]{1,0:T(8,128)(2,1)}, bf16[512,250]{1,0:T(8,128)(2,1)S(1)}, u32[]{:S(2)}, u32[]{:S(2)}) collective-permute-start(bf16[512,250]{1,0:T(8,128)(2,1)} %rest_0_.1), channel_id=1, source_target_pairs={{0,1},{1,0},{2,3},{3,2},{4,5},{5,4},{6,7},{7,6},{8,9},{9,8},{10,11... | collective-permute-start | bytes 768008 | tf_op jit(solution)/shard_map/ppermute | solution.py:245
  4.3 1.2 copy-start.1
  5.5 0.9 copy-start.2
  6.4 0.7 copy-start.3
  7.1 13.6 %copy-start = (f32[128,4008]{0,1:T(8,128)S(1)}, f32[128,4008]{0,1:T(8,128)}, u32[]{:S(2)}) copy-start(f32[128,4008]{0,1:T(8,128)} %param.10) | copy-start | bytes 6156292
  7.1 13.6 %copy-start.4 = (s32[2048]{0:T(1024)S(1)}, s32[2048]{0:T(1024)}, u32[]{:S(2)}) copy-start(s32[2048]{0:T(1024)} %param.12) | copy-start | bytes 24580
  9.4 28.9 %all-to-all-start = ((bf16[64,8,1024]{2,1,0:T(8,128)(2,1)}), bf16[64,8,1024]{2,1,0:T(8,128)(2,1)S(1)}, u32[]{:S(2)}, u32[]{:S(2)}) async-start(bf16[64,8,1024]{2,1,0:T(8,128)(2,1)} %bitcast.7), calls=%async_computation | async-start | bytes 2097152 | tf_op jit(solution)/shard_map/all_to_all | solution.py:255
  34.2 1.9 %collective-permute-start = (bf16[16,8,1152]{2,1,0:T(8,128)(2,1)S(1)}, bf16[16,8,1152]{2,1,0:T(8,128)(2,1)S(1)}, u32[]{:S(2)}, u32[]{:S(2)}) collective-permute-start(bf16[16,8,1152]{2,1,0:T(8,128)(2,1)S(1)} %get-tuple-element.19), channel_id=1, source_target_pairs={{0,1},{1,0},{2,3},{3,2},{4,5},{5,4},{6,7},{7,6},{8,9},{9,8},{10,11... | collective-permute-start | bytes 884744 | tf_op jit(solution)/shard_map/ppermute | solution.py:278
  38.4 28.4 %slice-start = ((s8[16416768]{0:T(1024)(128)(4,1)}), s8[4194304]{0:T(1024)(128)(4,1)S(1)}, s32[]{:S(2)}) async-start(s8[16416768]{0:T(1024)(128)(4,1)} %bitcast.10), calls=%async_computation.7 | async-start | bytes 8388608
  50.8 16.0 %slice-start.1 = ((s8[16416768]{0:T(1024)(128)(4,1)}), s8[4194304]{0:T(1024)(128)(4,1)S(1)}, s32[]{:S(2)}) async-start(s8[16416768]{0:T(1024)(128)(4,1)} %bitcast.10), calls=%async_computation.8 | async-start | bytes 8388608
  50.8 16.0 %slice-start.2 = ((s8[16416768]{0:T(1024)(128)(4,1)}), s8[4194304]{0:T(1024)(128)(4,1)S(1)}, s32[]{:S(2)}) async-start(s8[16416768]{0:T(1024)(128)(4,1)} %bitcast.10), calls=%async_computation.9 | async-start | bytes 8388608
  50.8 16.0 %slice-start.3 = ((s8[16416768]{0:T(1024)(128)(4,1)}), s8[3833856]{0:T(1024)(128)(4,1)S(1)}, s32[]{:S(2)}) async-start(s8[16416768]{0:T(1024)(128)(4,1)} %bitcast.10), calls=%async_computation.10 | async-start | bytes 7667712
  50.8 16.0 %copy-start.5 = (s32[128]{0:T(128)S(1)}, s32[128]{0:T(128)}, u32[]{:S(2)}) copy-start(s32[128]{0:T(128)} %param.13) | copy-start | bytes 1540
  62.7 4.2 %collective-permute-start.3 = (bf16[16,8,1152]{2,1,0:T(8,128)(2,1)S(1)}, bf16[16,8,1152]{2,1,0:T(8,128)(2,1)S(1)}, u32[]{:S(2)}, u32[]{:S(2)}) collective-permute-start(bf16[16,8,1152]{2,1,0:T(8,128)(2,1)S(1)} %all_to_all.36.mine_gap_ref), channel_id=1, source_target_pairs={{0,1},{1,0},{2,3},{3,2},{4,5},{5,4},{6,7},{7,6},{8,9},{9,8},{10,11... | collective-permute-start | bytes 884744 | tf_op jit(solution)/shard_map/ppermute | solution.py:309
  75.8 1.7 %collective-permute-start.4 = (bf16[16,8,1152]{2,1,0:T(8,128)(2,1)S(1)}, bf16[16,8,1152]{2,1,0:T(8,128)(2,1)S(1)}, u32[]{:S(2)}, u32[]{:S(2)}) collective-permute-start(bf16[16,8,1152]{2,1,0:T(8,128)(2,1)S(1)} %get-tuple-element.25), channel_id=1, source_target_pairs={{0,1},{1,0},{2,3},{3,2},{4,5},{5,4},{6,7},{7,6},{8,9},{9,8},{10,11... | collective-permute-start | bytes 884744 | tf_op jit(solution)/shard_map/ppermute | solution.py:278
  100.2 4.2 %collective-permute-start.5 = (bf16[16,8,1152]{2,1,0:T(8,128)(2,1)S(1)}, bf16[16,8,1152]{2,1,0:T(8,128)(2,1)S(1)}, u32[]{:S(2)}, u32[]{:S(2)}) collective-permute-start(bf16[16,8,1152]{2,1,0:T(8,128)(2,1)S(1)} %all_to_all.38.mine_gap_ref), channel_id=1, source_target_pairs={{0,1},{1,0},{2,3},{3,2},{4,5},{5,4},{6,7},{7,6},{8,9},{9,8},{10,11... | collective-permute-start | bytes 884744 | tf_op jit(solution)/shard_map/ppermute | solution.py:309
  113.4 1.7 %collective-permute-start.6 = (bf16[16,8,1152]{2,1,0:T(8,128)(2,1)S(1)}, bf16[16,8,1152]{2,1,0:T(8,128)(2,1)S(1)}, u32[]{:S(2)}, u32[]{:S(2)}) collective-permute-start(bf16[16,8,1152]{2,1,0:T(8,128)(2,1)S(1)} %get-tuple-element.29), channel_id=1, source_target_pairs={{0,1},{1,0},{2,3},{3,2},{4,5},{5,4},{6,7},{7,6},{8,9},{9,8},{10,11... | collective-permute-start | bytes 884744 | tf_op jit(solution)/shard_map/ppermute | solution.py:278
  137.7 4.1 %collective-permute-start.7 = (bf16[16,8,1152]{2,1,0:T(8,128)(2,1)S(1)}, bf16[16,8,1152]{2,1,0:T(8,128)(2,1)S(1)}, u32[]{:S(2)}, u32[]{:S(2)}) collective-permute-start(bf16[16,8,1152]{2,1,0:T(8,128)(2,1)S(1)} %all_to_all.40.mine_gap_ref), channel_id=1, source_target_pairs={{0,1},{1,0},{2,3},{3,2},{4,5},{5,4},{6,7},{7,6},{8,9},{9,8},{10,11... | collective-permute-start | bytes 884744 | tf_op jit(solution)/shard_map/ppermute | solution.py:309

commit v2 on v1

--- a/solution.py
+++ b/solution.py
@@ -12,9 +12,10 @@
 CHIPS = ("rows", "x", "y")
 LANES = 128
 CHUNK = 512
-AHEAD = 2
+AHEAD = 3
 epsilon = 1e-06
 step_size = 2.0
+
 
 def grant(mebibytes):
     return pltpu.CompilerParams(vmem_limit_bytes=mebibytes * 1024 * 1024)
@@ -35,10 +36,6 @@
     rest = value - high
     middle = rest.astype(jnp.bfloat16).astype(jnp.float32)
     return high, middle, rest - middle
-
-
-def matmul_nt(left, right):
-    return lax.dot_general(left, right, (((1,), (1,)), ((), ())), preferred_element_type=jnp.float32)
 
 
 def with_self(block, tokens, start):
@@ -77,14 +74,14 @@
         out_ref[:, :, half:] = stats
 
 
-def first_kernel(place_ref, tokens_ref, anchors_ref, logits_hbm, held_ref, mine_ref, other_ref, buffer, logits_ref, mass_ref, sem_in, sem_out, sem_base):
-    extent, rows = logits_ref.shape
+def first_kernel(place_ref, tokens_ref, anchors_ref, logits_hbm, held_ref, turned_ref, mine_ref, other_ref, logits_ref, mass_ref, sems, sem_base):
+    extent = logits_ref.shape[0]
     base = pltpu.make_async_copy(logits_hbm, logits_ref, sem_base)
     base.start()
-    loads, stores = [], []
+    loads = []
     for i, (start, size) in enumerate(chunks_of(extent)):
         where = pl.ds(start, size)
-        loads.append(pltpu.make_async_copy(anchors_ref.at[where], buffer.at[where], sem_in.at[i]))
+        loads.append(pltpu.make_async_copy(anchors_ref.at[where], held_ref.at[where], sems.at[i]))
     for load in loads[:AHEAD]:
         load.start()
     shifted = tokens_ref[...] - place_ref[0]
@@ -98,15 +95,12 @@
         loads[i].wait()
         if i + AHEAD < len(loads):
             loads[i + AHEAD].start()
-        buffer[where, :] = with_self(buffer[where, :], tokens, start)
-        store = pltpu.make_async_copy(buffer.at[where], held_ref.at[where], sem_out.at[i])
-        store.start()
-        stores.append(store)
-        return buffer[where, :]
+        block = with_self(held_ref[where, :], tokens, start)
+        held_ref[where, :] = block
+        turned_ref[:, start : start + size] = block.T
+        return held_ref[where, :]
 
     put_masses(place_ref[1], logits_ref, anchors_of, mine_ref, other_ref, mass_ref)
-    for store in stores:
-        store.wait()
 
 
 def lane_sum(stats, which):
@@ -123,8 +117,13 @@
     return tile.astype(jnp.bfloat16)
 
 
-def pair_kernel(mine_ref, other_ref, out_ref):
-    half = out_ref.shape[2] - LANES
+def pair_kernel(mine_ref, other_ref, *rest):
+    out_ref = rest[-1]
+    groups, eight, width = mine_ref.shape
+    half = width - LANES
+    if len(rest) > 1:
+        target = sum(ref[...].astype(jnp.float32) for ref in rest[:-1])
+        out_ref[:, :, width:] = target.reshape(groups, eight, half).astype(jnp.bfloat16)
     stats = [ref[:, :, half:].astype(jnp.float32) for ref in (mine_ref, other_ref)]
     tops = [lane_sum(stat, 0) for stat in stats]
     top = jnp.maximum(*tops)
@@ -133,17 +132,22 @@
     mine = mine_ref[:, :, :half].astype(jnp.float32) * factors[0]
     other = other_ref[:, :, :half].astype(jnp.float32) * factors[1]
     out_ref[:, :, :half] = (mine + other).astype(jnp.bfloat16)
-    out_ref[:, :, half:] = lane_tile(stats[0].shape, (top, total))
-
-
-def owner_kernel(full_vocab, first, in_ref, target_ref, out_ref, sum_ref=None):
-    half = in_ref.shape[2] - LANES
+    out_ref[:, :, half:width] = lane_tile(stats[0].shape, (top, total))
+
+
+def owner_kernel(full_vocab, first, in_ref, *rest):
     if first:
-        target = jnp.sum(target_ref[...].astype(jnp.float32), axis=0)
+        out_ref, sum_ref = rest
+    else:
+        target_ref, out_ref = rest
+    width = out_ref.shape[2]
+    half = width - LANES
+    if first:
+        target = jnp.sum(in_ref[:, :, width:].astype(jnp.float32), axis=0)
         sum_ref[...] = target
     else:
         target = target_ref[...]
-    stats = in_ref[:, :, half:].astype(jnp.float32)
+    stats = in_ref[:, :, half:width].astype(jnp.float32)
     top = lane_sum(stats, 0)
     row_max = jnp.max(top, axis=0, keepdims=True)
     factor = jnp.exp(top - row_max)
@@ -158,11 +162,11 @@
     out_ref[:, :, half:] = jnp.broadcast_to(tile[None], (in_ref.shape[0],) + tile.shape)
 
 
-def step_kernel(last, place_ref, mine_gap_ref, other_gap_ref, active_ref, base_ref, update_ref, held_ref, *rest):
+def step_kernel(last, place_ref, mine_gap_ref, other_gap_ref, active_ref, base_ref, update_ref, turned_ref, *rest):
     if last:
         new_ref, gap_all = rest
     else:
-        new_ref, mine_ref, other_ref, gap_all, logits_ref, mass_ref = rest
+        held_ref, new_ref, mine_ref, other_ref, gap_all, logits_ref, mass_ref = rest
     extent, rows = base_ref.shape
     half = mine_gap_ref.shape[2] - LANES
     core = place_ref[1]
@@ -184,7 +188,8 @@
     active = active_ref[...].astype(jnp.float32)
     for start, size in chunks_of(extent):
         where = pl.ds(start, size)
-        back = matmul_nt(held_ref[where, :], gap_all[...]) * scale
+        turned = jnp.dot(gap_all[...], turned_ref[:, start : start + size], preferred_element_type=jnp.float32)
+        back = turned.T * scale
         logits = base_ref[where, :]
         if update_ref is not None:
             logits = logits + update_ref[where, :]
@@ -198,26 +203,39 @@
 
 
 def no_update(kernel):
-    def run(place_ref, mine_gap_ref, other_gap_ref, active_ref, base_ref, held_ref, *rest):
-        kernel(place_ref, mine_gap_ref, other_gap_ref, active_ref, base_ref, None, held_ref, *rest)
+    def run(place_ref, mine_gap_ref, other_gap_ref, active_ref, base_ref, turned_ref, *rest):
+        kernel(place_ref, mine_gap_ref, other_gap_ref, active_ref, base_ref, None, turned_ref, *rest)
 
     return run
 
 
-def target_kernel(place_ref, tokens_ref, *rest):
-    out_ref = rest[-1]
-    half = out_ref.shape[1]
+def target_kernel(place_ref, *rest):
+    *rest, total_ref, sems = rest
+    sources, outs, (tokens_ref, *buffers) = rest[:5], rest[5:-5], rest[-5:]
+    copies = [
+        pltpu.make_async_copy(source, buffer, sems.at[i])
+        for i, (source, buffer) in enumerate(zip(sources, (tokens_ref, *buffers)))
+    ]
+    for copy in copies:
+        copy.start()
+    rows, half = outs[0].shape
     columns = pl.ds(pl.multiple_of(place_ref[0] * half, half), half)
+    copies[0].wait()
     tokens = tokens_ref[:, columns]
     total = None
     for i in range(2):
-        delta_ref, anchors_ref = rest[2 * i : 2 * i + 2]
+        for copy in copies[1 + 2 * i : 3 + 2 * i]:
+            copy.wait()
+        delta_ref, anchors_ref = buffers[2 * i : 2 * i + 2]
         block = anchors_ref[:, columns].astype(jnp.float32)
         place = lax.broadcasted_iota(jnp.int32, block.shape, 0) + place_ref[1 + i]
         block = jnp.where(place == tokens, block + 1.0, block).astype(jnp.bfloat16)
         part = jnp.dot(delta_ref[...], block, preferred_element_type=jnp.float32)
         total = part if total is None else total + part
-    out_ref[...] = total.astype(jnp.bfloat16)
+    total_ref[...] = total
+    for far, out_ref in enumerate(outs):
+        group = lax.rem(place_ref[3] + far, len(outs))
+        out_ref[...] = total_ref[pl.ds(pl.multiple_of(group * rows, rows), rows), :].astype(jnp.bfloat16)
 
 
 def shards(expert_delta, small_anchors, small_tokens, base_logits, base_anchors, base_tokens, active_rows):
@@ -235,7 +253,7 @@
     pieces = len(chunks_of(base_width))
 
     core = lax.axis_index("core")
-    small_place = jnp.stack([core, place * small_width, (place + 1 - 2 * core) * small_width])
+    small_place = jnp.stack([core, place * small_width, (place + 1 - 2 * core) * small_width, lax.axis_index("rows")])
     base_place = jnp.stack([vocab_place * base_width, core])
     small_tokens, base_tokens = small_tokens[None, :], base_tokens[None, :]
     active = active_rows[None, :]
@@ -244,48 +262,60 @@
     swap = [(0, 1), (1, 0)]
     other_delta = lax.ppermute(expert_delta, "core", swap)
     other_anchors = lax.ppermute(small_anchors, "core", swap)
-    target = pl.pallas_call(
+    row_groups = lax.axis_size("rows")
+    targets = pl.pallas_call(
         target_kernel,
-        out_shape=jax.ShapeDtypeStruct((all_rows, half), bf16),
-        in_specs=[SMEM, VMEM, VMEM, VMEM, VMEM, VMEM],
-        out_specs=VMEM,
-        compiler_params=grant(16),
+        out_shape=(jax.ShapeDtypeStruct((rows, half), bf16),) * row_groups,
+        in_specs=[SMEM] + [HBM] * 5,
+        out_specs=(VMEM,) * row_groups,
+        scratch_shapes=[pltpu.VMEM(small_tokens.shape, jnp.int32)]
+        + [pltpu.VMEM(each.shape, bf16) for each in (expert_delta, small_anchors)] * 2
+        + [pltpu.VMEM((all_rows, half), f32), pltpu.SemaphoreType.DMA((5,))],
+        compiler_params=grant(20),
         name="target_parts",
-    )(small_place, small_tokens, expert_delta, small_anchors, other_delta, other_anchors)
-    target = lax.all_to_all(target.reshape(-1, eight, half), CHIPS, 0, 0, tiled=True)
+    )(
+        small_place,
+        *(pltpu.with_memory_space_constraint(each, pltpu.HBM) for each in (small_tokens, expert_delta, small_anchors)),
+        other_delta,
+        other_anchors,
+    )
+    base_place, base_tokens, targets = lax.optimization_barrier((base_place, base_tokens, list(targets)))
+    for far in range(1, row_groups):
+        ring = [(i, (i + far) % row_groups) for i in range(row_groups)]
+        targets[far] = lax.ppermute(targets[far], "rows", ring)
 
     sent_shape = jax.ShapeDtypeStruct((groups, eight, width), bf16)
-    held_shape = jax.ShapeDtypeStruct((base_width, anchors), bf16)
+    held_shape = pltpu.VMEM((base_width, anchors), bf16)
+    turned_shape = pltpu.VMEM((anchors, -(-base_width // LANES) * LANES), bf16)
     update_shape = jax.ShapeDtypeStruct((base_width, rows), f32)
-    held, mine, other = pl.pallas_call(
+    held, turned, mine, other = pl.pallas_call(
         first_kernel,
-        out_shape=(held_shape, sent_shape, sent_shape),
+        out_shape=(held_shape, turned_shape, sent_shape, sent_shape),
         in_specs=[SMEM, VMEM, HBM, HBM],
-        out_specs=(HBM, VMEM, VMEM),
+        out_specs=(VMEM,) * 4,
         scratch_shapes=[
-            pltpu.VMEM((base_width, anchors), bf16),
             pltpu.VMEM((base_width, rows), f32),
             pltpu.VMEM((rows, anchors), f32),
             pltpu.SemaphoreType.DMA((pieces,)),
-            pltpu.SemaphoreType.DMA((pieces,)),
             pltpu.SemaphoreType.DMA,
         ],
-        compiler_params=grant(36),
+        compiler_params=grant(23),
+        cost_estimate=pl.CostEstimate(flops=8_000_000_000, bytes_accessed=40_000_000, transcendentals=base_width * rows),
         name="first_masses",
     )(base_place, base_tokens, base_anchors, base)
 
-    def both(mine, other):
+    def both(mine, other, *more):
         other = lax.ppermute(other, "core", swap)
         return pl.pallas_call(
             pair_kernel,
-            out_shape=sent_shape,
-            in_specs=[VMEM, VMEM],
+            out_shape=jax.ShapeDtypeStruct((groups, eight, width + (half if more else 0)), bf16),
+            in_specs=[VMEM] * (2 + len(more)),
             out_specs=VMEM,
-            compiler_params=grant(4),
+            compiler_params=grant(5),
             name="pair",
-        )(mine, other)
-
-    sent, target = lax.optimization_barrier((both(mine, other), target))
+        )(mine, other, *more)
+
+    sent = both(mine, other, *targets)
     update = None
     for turn in range(ITERATIONS):
         last = turn == ITERATIONS - 1
@@ -295,12 +325,11 @@
         result = pl.pallas_call(
             functools.partial(owner_kernel, float(base_width * vocab_count), first),
             out_shape=(sent_shape, target_shape) if first else sent_shape,
-            in_specs=[VMEM, VMEM],
+            in_specs=[VMEM] if first else [VMEM, VMEM],
             out_specs=(VMEM, VMEM) if first else VMEM,
             compiler_params=grant(4),
-            cost_estimate=pl.CostEstimate(flops=20_000_000_000, bytes_accessed=40_000_000, transcendentals=0) if first else None,
             name="owner",
-        )(got, target)
+        )(*((got,) if first else (got, target)))
         if first:
             copies, target = result
         else:
@@ -308,7 +337,7 @@
         gaps = lax.all_to_all(copies, CHIPS[1:], 0, 0, tiled=True)
         other_gaps = lax.ppermute(gaps, "core", swap)
         kernel = functools.partial(step_kernel, last)
-        operands = [base_place, gaps, other_gaps, active, base] + ([] if update is None else [update]) + [held]
+        operands = [base_place, gaps, other_gaps, active, base] + ([] if update is None else [update]) + [turned] + ([] if last else [held])
         result = pl.pallas_call(
             no_update(kernel) if update is None else kernel,
             out_shape=update_shape if last else (update_shape, sent_shape, sent_shape),
@@ -316,7 +345,7 @@
             out_specs=VMEM if last else (VMEM, VMEM, VMEM),
             scratch_shapes=[pltpu.VMEM((rows, anchors), bf16)]
             + ([] if last else [pltpu.VMEM((base_width, rows), f32), pltpu.VMEM((rows, anchors), f32)]),
-            compiler_params=grant(16),
+            compiler_params=grant(7),
             name="step",
         )(*operands)
         if last:
@@ -339,4 +368,5 @@
         P(),
         P("rows"),
     )
+
     return jax.shard_map(shards, mesh=split, in_specs=in_specs, out_specs=P("rows", VOCAB), check_vma=False)

time: 149 us -> 146 us (0.980)
  waiting for transfers between devices: 12.1 us -> 19.3 us
  Pallas kernels: 41.8 us -> 34.6 us
  starting transfers between devices: 23.1 us -> 18 us
  blocking collectives: 68.2 us -> 72.2 us
  local copies, waits for them, and re-layouts: 2.9 us -> 0.97 us
    all_to_all x1 -> x0, starting transfers between devices: 11.2 us -> none  [shards(): lax.all_to_all(target.reshape(-1, eight, half), CHIPS, 0, 0, tiled=True)]
    ppermute x0 -> x3, waiting for transfers between devices: none -> 11.1 us  [shards(): targets[far] = lax.ppermute(targets[far], 'rows', ring)]
    pallas_call x3, Pallas kernels: 24.4 us -> 17.3 us  [shards(): pl.pallas_call(no_update(kernel) if update is None else kernel, out_shape...]
    ppermute x0 -> x3, starting transfers between devices: none -> 5.78 us  [shards(): targets[far] = lax.ppermute(targets[far], 'rows', ring)]
    all_to_all x3, blocking collectives: 34.2 us -> 39 us  [shards(): got = lax.all_to_all(sent, CHIPS[1:], 0, 0, tiled=True)]
    all_to_all x1 -> x0, waiting for transfers between devices: 2.01 us -> none  [shards(): lax.all_to_all(target.reshape(-1, eight, half), CHIPS, 0, 0, tiled=True)]
    unnamed x20 -> x8, local copies, waits for them, and re-layouts: 2.9 us -> 0.97 us
  transfers between devices with their start and end apart: 9 -> 11, of which waited for: 8 -> 8; matrix products, arithmetic and copies ran while one was open for 0% -> 0% of each run, Pallas kernels for 9% -> 0%
where the time goes in v2:
time: 146 us
  blocking collectives  72.2 us (49%)
  Pallas kernels  34.6 us (24%)
  waiting for transfers between devices  19.3 us (13%)
  starting transfers between devices  18 us (12%)
    all_to_all x3, blocking collectives, shards(): got = lax.all_to_all(sent, CHIPS[1:], 0, 0, tiled=True)  39 us
    all_to_all x3, blocking collectives, shards(): gaps = lax.all_to_all(copies, CHIPS[1:], 0, 0, tiled=True)  33.2 us
    pallas_call x3, Pallas kernels, shards(): pl.pallas_call(no_update(kernel) if update is None else kernel, out_shape...  17.3 us
    pallas_call x1, Pallas kernels, shards(): pl.pallas_call(first_kernel, out_shape=(held_shape, turned_shape, sent_sh...  12.3 us
    ppermute x3, waiting for transfers between devices, shards(): targets[far] = lax.ppermute(targets[far], 'rows', ring)  11.1 us
    ppermute x3, starting transfers between devices, shards(): other_gaps = lax.ppermute(gaps, 'core', swap)  9.43 us
    ppermute x3, starting transfers between devices, shards(): targets[far] = lax.ppermute(targets[far], 'rows', ring)  5.78 us
    ppermute x3, waiting for transfers between devices, shards(): other_gaps = lax.ppermute(gaps, 'core', swap)  3.63 us
  transfers between devices with their start and end apart: 11, of which 8 were waited for; matrix products, arithmetic and copies ran while one was open for 0% of the time, Pallas kernels for 0%

profile of v2, /device:TPU:1, one launch (start us, length us, event | category | flops | bytes accessed | tf_op | source)
XLA Modules:
  0.0 145.8 jit_solution(17255497811754600263)
XLA Ops:
  0.0 1.4 collective-permute-start.1
  1.4 0.0 collective-permute-start
  1.4 0.7 pad_add_fusion.place_ref
  2.0 0.1 pad_add_fusion.1.place_ref
  2.1 2.1 %collective-permute-done.rest_3_ = bf16[512,250]{1,0:T(8,128)(2,1)S(1)} collective-permute-done((bf16[512,250]{1,0:T(8,128)(2,1)}, bf16[512,250]{1,0:T(8,128)(2,1)S(1)}, u32[]{:S(2)}, u32[]{:S(2)}) %collective-permute-start) | collective-permute-done | bytes 256032 | tf_op jit(solution)/shard_map/ppermute | solution.py:263
  4.3 0.0 collective-permute-done.1.rest_4_
  4.3 3.2 %target_parts.1 = (bf16[128,1024]{1,0:T(8,128)(2,1)S(1)}, bf16[128,1024]{1,0:T(8,128)(2,1)S(1)}, bf16[128,1024]{1,0:T(8,128)(2,1)S(1)}, bf16[128,1024]{1,0:T(8,128)(2,1)S(1)}) custom-call(s32[4]{0:T(128)S(1)} %pad_add_fusion.1.place_ref, s32[1,2048]{1,0:T(1,128)} %bitcast.17, bf16[512,250]{1,0:T(8,128)(2,1)} %rest_1_.1, bf16[250,2048]{1,0:T(8,128)(2,1)} %rest_2_.1, ...), custom_call_target="tpu_custom_call" | custom-call | tf_op jit(solution)/shard_map/target_parts/pallas_call | solution.py:266
  7.4 12.3 %first_masses.1 = (bf16[4008,2048]{1,0:T(8,128)(2,1)S(1)}, bf16[2048,4096]{1,0:T(8,128)(2,1)S(1)}, bf16[16,8,1152]{2,1,0:T(8,128)(2,1)}, bf16[16,8,1152]{2,1,0:T(8,128)(2,1)}) custom-call(s32[2]{0:T(128)} %pad_add_fusion.place_ref, s32[1,2048]{1,0:T(1,128)} %bitcast.18, bf16[4008,2048]{1,0:T(8,128)(2,1)} %anchors_ref.1, f32[4008,128]{1,0:T(8,128)} %bitcast.10), custom_call_target="tpu_custom_call" | custom-call | flops 8000000000 | bytes 40000000 | tf_op jit(solution)/shard_map/first_masses/pallas_call | solution.py:291
  19.8 0.5 collective-permute-start.2
  20.2 1.8 %collective-permute-start.3 = (bf16[128,1024]{1,0:T(8,128)(2,1)S(1)}, bf16[128,1024]{1,0:T(8,128)(2,1)S(1)}, u32[]{:S(2)}, u32[]{:S(2)}) collective-permute-start(bf16[128,1024]{1,0:T(8,128)(2,1)S(1)} %get-tuple-element.36), channel_id=1, source_target_pairs={{0,32},{32,64},{64,96},{96,0},{1,33},{33,65},{65,97},{97,1},{2,34}... | collective-permute-start | bytes 786440 | tf_op jit(solution)/shard_map/ppermute | solution.py:285
  22.0 3.3 %collective-permute-start.4 = (bf16[128,1024]{1,0:T(8,128)(2,1)S(1)}, bf16[128,1024]{1,0:T(8,128)(2,1)S(1)}, u32[]{:S(2)}, u32[]{:S(2)}) collective-permute-start(bf16[128,1024]{1,0:T(8,128)(2,1)S(1)} %get-tuple-element.37), channel_id=1, source_target_pairs={{0,64},{32,96},{64,0},{96,32},{1,65},{33,97},{65,1},{97,33},{2,66}... | collective-permute-start | bytes 786440 | tf_op jit(solution)/shard_map/ppermute | solution.py:285
  25.3 0.7 collective-permute-start.5
  26.0 4.6 %collective-permute-done.3.rest_1_ = bf16[128,1024]{1,0:T(8,128)(2,1)S(1)} collective-permute-done((bf16[128,1024]{1,0:T(8,128)(2,1)S(1)}, bf16[128,1024]{1,0:T(8,128)(2,1)S(1)}, u32[]{:S(2)}, u32[]{:S(2)}) %collective-permute-start.3) | collective-permute-done | bytes 262176 | tf_op jit(solution)/shard_map/ppermute | solution.py:285
  30.6 6.5 %collective-permute-done.4.rest_2_ = bf16[128,1024]{1,0:T(8,128)(2,1)S(1)} collective-permute-done((bf16[128,1024]{1,0:T(8,128)(2,1)S(1)}, bf16[128,1024]{1,0:T(8,128)(2,1)S(1)}, u32[]{:S(2)}, u32[]{:S(2)}) %collective-permute-start.4) | collective-permute-done | bytes 262176 | tf_op jit(solution)/shard_map/ppermute | solution.py:285
  37.2 0.0 collective-permute-done.5.rest_3_
  37.2 0.0 collective-permute-done.2.other_ref
  37.2 0.0 copy-start.1
  37.2 1.0 copy-done.1
  38.1 0.0 copy-start
  38.1 0.0 copy-start.2
  38.1 0.0 copy-start.3
  38.1 0.5 pair.3
  38.6 17.1 %all_to_all.30.in_ref = bf16[16,8,2176]{2,1,0:T(8,128)(2,1)S(1)} all-to-all(bf16[16,8,2176]{2,1,0:T(8,128)(2,1)S(1)} %pair.3), channel_id=1, replica_groups=mesh['rows'=4,'x'=4,'y'=4,'core'=2] {'x','y'}, dimensions={0} | all-to-all | bytes 1114112 | tf_op jit(solution)/shard_map/all_to_all | solution.py:322
  55.7 0.3 owner.3
  56.0 10.8 %all_to_all.31.mine_gap_ref = bf16[16,8,1152]{2,1,0:T(8,128)(2,1)S(1)} all-to-all(bf16[16,8,1152]{2,1,0:T(8,128)(2,1)S(1)} %get-tuple-element.39), channel_id=1, replica_groups=mesh['rows'=4,'x'=4,'y'=4,'core'=2] {'x','y'}, dimensions={0} | all-to-all | bytes 589824 | tf_op jit(solution)/shard_map/all_to_all | solution.py:337
  66.8 3.6 %collective-permute-start.6 = (bf16[16,8,1152]{2,1,0:T(8,128)(2,1)S(1)}, bf16[16,8,1152]{2,1,0:T(8,128)(2,1)S(1)}, u32[]{:S(2)}, u32[]{:S(2)}) collective-permute-start(bf16[16,8,1152]{2,1,0:T(8,128)(2,1)S(1)} %all_to_all.31.mine_gap_ref), channel_id=1, source_target_pairs={{0,1},{1,0},{2,3},{3,2},{4,5},{5,4},{6,7},{7,6},{8,9},{9,8},{10,11... | collective-permute-start | bytes 884744 | tf_op jit(solution)/shard_map/ppermute | solution.py:338
  70.3 1.2 collective-permute-done.6.other_gap_ref
  71.5 0.0 copy-done
  71.5 0.0 copy-done.2
  71.5 0.0 copy-done.3
  71.5 6.2 %step.3 = (f32[4008,128]{1,0:T(8,128)S(1)}, bf16[16,8,1152]{2,1,0:T(8,128)(2,1)S(1)}, bf16[16,8,1152]{2,1,0:T(8,128)(2,1)S(1)}) custom-call(s32[2]{0:T(128)S(1)} %copy-done.3, bf16[16,8,1152]{2,1,0:T(8,128)(2,1)S(1)} %all_to_all.31.mine_gap_ref, bf16[16,8,1152]{2,1,0:T(8,128)(2,1)S(1)} %collective-permute-done.6.other_gap_ref, s32[1,128]{1,0:T(1,128)S(1)} %bitcast.14, ...), custom_call_target="tpu_custom_call" | custom-call | tf_op jit(solution)/shard_map/step/pallas_call | solution.py:341
  77.7 0.5 collective-permute-start.7
  78.2 1.2 collective-permute-done.7.other_ref
  79.4 0.3 pair.4
  79.7 10.9 %all_to_all.32.in_ref = bf16[16,8,1152]{2,1,0:T(8,128)(2,1)S(1)} all-to-all(bf16[16,8,1152]{2,1,0:T(8,128)(2,1)S(1)} %pair.4), channel_id=1, replica_groups=mesh['rows'=4,'x'=4,'y'=4,'core'=2] {'x','y'}, dimensions={0} | all-to-all | bytes 589824 | tf_op jit(solution)/shard_map/all_to_all | solution.py:322
  90.6 0.3 owner.4
  90.8 11.2 %all_to_all.33.mine_gap_ref = bf16[16,8,1152]{2,1,0:T(8,128)(2,1)S(1)} all-to-all(bf16[16,8,1152]{2,1,0:T(8,128)(2,1)S(1)} %owner.4), channel_id=1, replica_groups=mesh['rows'=4,'x'=4,'y'=4,'core'=2] {'x','y'}, dimensions={0} | all-to-all | bytes 589824 | tf_op jit(solution)/shard_map/all_to_all | solution.py:337
  102.0 2.9 %collective-permute-start.8 = (bf16[16,8,1152]{2,1,0:T(8,128)(2,1)S(1)}, bf16[16,8,1152]{2,1,0:T(8,128)(2,1)S(1)}, u32[]{:S(2)}, u32[]{:S(2)}) collective-permute-start(bf16[16,8,1152]{2,1,0:T(8,128)(2,1)S(1)} %all_to_all.33.mine_gap_ref), channel_id=1, source_target_pairs={{0,1},{1,0},{2,3},{3,2},{4,5},{5,4},{6,7},{7,6},{8,9},{9,8},{10,11... | collective-permute-start | bytes 884744 | tf_op jit(solution)/shard_map/ppermute | solution.py:338
  105.0 1.2 collective-permute-done.8.other_gap_ref
  106.2 6.3 %step.4 = (f32[4008,128]{1,0:T(8,128)S(1)}, bf16[16,8,1152]{2,1,0:T(8,128)(2,1)S(1)}, bf16[16,8,1152]{2,1,0:T(8,128)(2,1)S(1)}) custom-call(s32[2]{0:T(128)S(1)} %copy-done.3, bf16[16,8,1152]{2,1,0:T(8,128)(2,1)S(1)} %all_to_all.33.mine_gap_ref, bf16[16,8,1152]{2,1,0:T(8,128)(2,1)S(1)} %collective-permute-done.8.other_gap_ref, s32[1,128]{1,0:T(1,128)S(1)} %bitcast.15, ...), custom_call_target="tpu_custom_call" | custom-call | tf_op jit(solution)/shard_map/step/pallas_call | solution.py:341
  112.5 0.5 collective-permute-start.9
  113.0 1.2 collective-permute-done.9.other_ref
  114.2 0.3 pair.5
  114.5 10.9 %all_to_all.34.in_ref = bf16[16,8,1152]{2,1,0:T(8,128)(2,1)S(1)} all-to-all(bf16[16,8,1152]{2,1,0:T(8,128)(2,1)S(1)} %pair.5), channel_id=1, replica_groups=mesh['rows'=4,'x'=4,'y'=4,'core'=2] {'x','y'}, dimensions={0} | all-to-all | bytes 589824 | tf_op jit(solution)/shard_map/all_to_all | solution.py:322
  125.4 0.3 owner.5
  125.6 11.2 %all_to_all.35.mine_gap_ref = bf16[16,8,1152]{2,1,0:T(8,128)(2,1)S(1)} all-to-all(bf16[16,8,1152]{2,1,0:T(8,128)(2,1)S(1)} %owner.5), channel_id=1, replica_groups=mesh['rows'=4,'x'=4,'y'=4,'core'=2] {'x','y'}, dimensions={0} | all-to-all | bytes 589824 | tf_op jit(solution)/shard_map/all_to_all | solution.py:337
  136.9 2.9 %collective-permute-start.10 = (bf16[16,8,1152]{2,1,0:T(8,128)(2,1)S(1)}, bf16[16,8,1152]{2,1,0:T(8,128)(2,1)S(1)}, u32[]{:S(2)}, u32[]{:S(2)}) collective-permute-start(bf16[16,8,1152]{2,1,0:T(8,128)(2,1)S(1)} %all_to_all.35.mine_gap_ref), channel_id=1, source_target_pairs={{0,1},{1,0},{2,3},{3,2},{4,5},{5,4},{6,7},{7,6},{8,9},{9,8},{10,11... | collective-permute-start | bytes 884744 | tf_op jit(solution)/shard_map/ppermute | solution.py:338
  139.8 1.2 collective-permute-done.10.other_gap_ref
  141.0 4.8 %step.5 = f32[4008,128]{1,0:T(8,128)} custom-call(s32[2]{0:T(128)S(1)} %copy-done.3, bf16[16,8,1152]{2,1,0:T(8,128)(2,1)S(1)} %all_to_all.35.mine_gap_ref, bf16[16,8,1152]{2,1,0:T(8,128)(2,1)S(1)} %collective-permute-done.10.other_gap_ref, s32[1,128]{1,0:T(1,128)S(1)} %bitcast.16, f32[4008,128]{1,0:T(8,128)S(1)} %bitcast.13, ...), custom_call_target="tpu_custom_call" | custom-call | tf_op jit(solution)/shard_map/step/pallas_call | solution.py:341
Async XLA Ops:
  0.0 4.3 %collective-permute-start.1 = (bf16[250,2048]{1,0:T(8,128)(2,1)}, bf16[250,2048]{1,0:T(8,128)(2,1)S(1)}, u32[]{:S(2)}, u32[]{:S(2)}) collective-permute-start(bf16[250,2048]{1,0:T(8,128)(2,1)} %rest_2_.1), channel_id=1, source_target_pairs={{0,1},{1,0},{2,3},{3,2},{4,5},{5,4},{6,7},{7,6},{8,9},{9,8},{10,11... | collective-permute-start | bytes 3072008 | tf_op jit(solution)/shard_map/ppermute | solution.py:264
  1.4 2.9 %collective-permute-start = (bf16[512,250]{1,0:T(8,128)(2,1)}, bf16[512,250]{1,0:T(8,128)(2,1)S(1)}, u32[]{:S(2)}, u32[]{:S(2)}) collective-permute-start(bf16[512,250]{1,0:T(8,128)(2,1)} %rest_1_.1), channel_id=1, source_target_pairs={{0,1},{1,0},{2,3},{3,2},{4,5},{5,4},{6,7},{7,6},{8,9},{9,8},{10,11... | collective-permute-start | bytes 768008 | tf_op jit(solution)/shard_map/ppermute | solution.py:263
  19.8 17.4 %collective-permute-start.2 = (bf16[16,8,1152]{2,1,0:T(8,128)(2,1)}, bf16[16,8,1152]{2,1,0:T(8,128)(2,1)S(1)}, u32[]{:S(2)}, u32[]{:S(2)}) collective-permute-start(bf16[16,8,1152]{2,1,0:T(8,128)(2,1)} %get-tuple-element.34), channel_id=1, source_target_pairs={{0,1},{1,0},{2,3},{3,2},{4,5},{5,4},{6,7},{7,6},{8,9},{9,8},{10,11... | collective-permute-start | bytes 884744 | tf_op jit(solution)/shard_map/ppermute | solution.py:308
  20.2 10.4 %collective-permute-start.3 = (bf16[128,1024]{1,0:T(8,128)(2,1)S(1)}, bf16[128,1024]{1,0:T(8,128)(2,1)S(1)}, u32[]{:S(2)}, u32[]{:S(2)}) collective-permute-start(bf16[128,1024]{1,0:T(8,128)(2,1)S(1)} %get-tuple-element.36), channel_id=1, source_target_pairs={{0,32},{32,64},{64,96},{96,0},{1,33},{33,65},{65,97},{97,1},{2,34}... | collective-permute-start | bytes 786440 | tf_op jit(solution)/shard_map/ppermute | solution.py:285
  22.0 15.2 %collective-permute-start.4 = (bf16[128,1024]{1,0:T(8,128)(2,1)S(1)}, bf16[128,1024]{1,0:T(8,128)(2,1)S(1)}, u32[]{:S(2)}, u32[]{:S(2)}) collective-permute-start(bf16[128,1024]{1,0:T(8,128)(2,1)S(1)} %get-tuple-element.37), channel_id=1, source_target_pairs={{0,64},{32,96},{64,0},{96,32},{1,65},{33,97},{65,1},{97,33},{2,66}... | collective-permute-start | bytes 786440 | tf_op jit(solution)/shard_map/ppermute | solution.py:285
  25.3 11.9 %collective-permute-start.5 = (bf16[128,1024]{1,0:T(8,128)(2,1)S(1)}, bf16[128,1024]{1,0:T(8,128)(2,1)S(1)}, u32[]{:S(2)}, u32[]{:S(2)}) collective-permute-start(bf16[128,1024]{1,0:T(8,128)(2,1)S(1)} %get-tuple-element.38), channel_id=1, source_target_pairs={{0,96},{32,0},{64,32},{96,64},{1,97},{33,1},{65,33},{97,65},{2,98}... | collective-permute-start | bytes 786440 | tf_op jit(solution)/shard_map/ppermute | solution.py:285
  37.2 1.0 copy-start.1
  38.1 33.4 %copy-start = (f32[128,4008]{0,1:T(8,128)S(1)}, f32[128,4008]{0,1:T(8,128)}, u32[]{:S(2)}) copy-start(f32[128,4008]{0,1:T(8,128)} %param.10) | copy-start | bytes 6156292
  38.1 33.4 %copy-start.2 = (s32[128]{0:T(128)S(1)}, s32[128]{0:T(128)}, u32[]{:S(2)}) copy-start(s32[128]{0:T(128)} %param.13) | copy-start | bytes 1540
  38.1 33.4 %copy-start.3 = (s32[2]{0:T(128)S(1)}, s32[2]{0:T(128)}, u32[]{:S(2)}) copy-start(s32[2]{0:T(128)} %pad_add_fusion.place_ref) | copy-start | bytes 28
  66.8 4.8 %collective-permute-start.6 = (bf16[16,8,1152]{2,1,0:T(8,128)(2,1)S(1)}, bf16[16,8,1152]{2,1,0:T(8,128)(2,1)S(1)}, u32[]{:S(2)}, u32[]{:S(2)}) collective-permute-start(bf16[16,8,1152]{2,1,0:T(8,128)(2,1)S(1)} %all_to_all.31.mine_gap_ref), channel_id=1, source_target_pairs={{0,1},{1,0},{2,3},{3,2},{4,5},{5,4},{6,7},{7,6},{8,9},{9,8},{10,11... | collective-permute-start | bytes 884744 | tf_op jit(solution)/shard_map/ppermute | solution.py:338
  77.7 1.7 %collective-permute-start.7 = (bf16[16,8,1152]{2,1,0:T(8,128)(2,1)S(1)}, bf16[16,8,1152]{2,1,0:T(8,128)(2,1)S(1)}, u32[]{:S(2)}, u32[]{:S(2)}) collective-permute-start(bf16[16,8,1152]{2,1,0:T(8,128)(2,1)S(1)} %get-tuple-element.43), channel_id=1, source_target_pairs={{0,1},{1,0},{2,3},{3,2},{4,5},{5,4},{6,7},{7,6},{8,9},{9,8},{10,11... | collective-permute-start | bytes 884744 | tf_op jit(solution)/shard_map/ppermute | solution.py:308
  102.0 4.2 %collective-permute-start.8 = (bf16[16,8,1152]{2,1,0:T(8,128)(2,1)S(1)}, bf16[16,8,1152]{2,1,0:T(8,128)(2,1)S(1)}, u32[]{:S(2)}, u32[]{:S(2)}) collective-permute-start(bf16[16,8,1152]{2,1,0:T(8,128)(2,1)S(1)} %all_to_all.33.mine_gap_ref), channel_id=1, source_target_pairs={{0,1},{1,0},{2,3},{3,2},{4,5},{5,4},{6,7},{7,6},{8,9},{9,8},{10,11... | collective-permute-start | bytes 884744 | tf_op jit(solution)/shard_map/ppermute | solution.py:338
  112.5 1.7 %collective-permute-start.9 = (bf16[16,8,1152]{2,1,0:T(8,128)(2,1)S(1)}, bf16[16,8,1152]{2,1,0:T(8,128)(2,1)S(1)}, u32[]{:S(2)}, u32[]{:S(2)}) collective-permute-start(bf16[16,8,1152]{2,1,0:T(8,128)(2,1)S(1)} %get-tuple-element.47), channel_id=1, source_target_pairs={{0,1},{1,0},{2,3},{3,2},{4,5},{5,4},{6,7},{7,6},{8,9},{9,8},{10,11... | collective-permute-start | bytes 884744 | tf_op jit(solution)/shard_map/ppermute | solution.py:308
  136.9 4.1 %collective-permute-start.10 = (bf16[16,8,1152]{2,1,0:T(8,128)(2,1)S(1)}, bf16[16,8,1152]{2,1,0:T(8,128)(2,1)S(1)}, u32[]{:S(2)}, u32[]{:S(2)}) collective-permute-start(bf16[16,8,1152]{2,1,0:T(8,128)(2,1)S(1)} %all_to_all.35.mine_gap_ref), channel_id=1, source_target_pairs={{0,1},{1,0},{2,3},{3,2},{4,5},{5,4},{6,7},{7,6},{8,9},{9,8},{10,11... | collective-permute-start | bytes 884744 | tf_op jit(solution)/shard_map/ppermute | solution.py:338

commit v3 on v2

--- a/solution.py
+++ b/solution.py
@@ -74,10 +74,8 @@
         out_ref[:, :, half:] = stats
 
 
-def first_kernel(place_ref, tokens_ref, anchors_ref, logits_hbm, held_ref, turned_ref, mine_ref, other_ref, logits_ref, mass_ref, sems, sem_base):
+def first_kernel(place_ref, tokens_ref, anchors_ref, logits_ref, held_ref, turned_ref, mine_ref, other_ref, mass_ref, sems):
     extent = logits_ref.shape[0]
-    base = pltpu.make_async_copy(logits_hbm, logits_ref, sem_base)
-    base.start()
     loads = []
     for i, (start, size) in enumerate(chunks_of(extent)):
         where = pl.ds(start, size)
@@ -87,7 +85,6 @@
     shifted = tokens_ref[...] - place_ref[0]
     shifted = jnp.where((shifted >= 0) & (shifted < extent), shifted, -1)
     tokens = jnp.broadcast_to(shifted, (16, shifted.shape[1])).astype(jnp.int16)
-    base.wait()
 
     def anchors_of(start, size):
         i = start // CHUNK
@@ -164,7 +161,7 @@
 
 def step_kernel(last, place_ref, mine_gap_ref, other_gap_ref, active_ref, base_ref, update_ref, turned_ref, *rest):
     if last:
-        new_ref, gap_all = rest
+        out_ref, new_ref, gap_all, sems = rest
     else:
         held_ref, new_ref, mine_ref, other_ref, gap_all, logits_ref, mass_ref = rest
     extent, rows = base_ref.shape
@@ -186,6 +183,7 @@
     scale = lax.rsqrt(squares / (2 * half) + epsilon)
     slope = scale * inner / total
     active = active_ref[...].astype(jnp.float32)
+    copies = []
     for start, size in chunks_of(extent):
         where = pl.ds(start, size)
         turned = jnp.dot(gap_all[...], turned_ref[:, start : start + size], preferred_element_type=jnp.float32)
@@ -196,8 +194,14 @@
         weights = jnp.exp(logits - row_max)
         change = -step_size * active * weights * (back - slope)
         new_ref[where, :] = change if update_ref is None else update_ref[where, :] + change
-        if not last:
+        if last:
+            copy = pltpu.make_async_copy(new_ref.at[where], out_ref.at[where], sems.at[len(copies)])
+            copy.start()
+            copies.append(copy)
+        else:
             logits_ref[where, :] = logits + change
+    for copy in copies:
+        copy.wait()
     if not last:
         put_masses(core, logits_ref, lambda start, size: held_ref[pl.ds(start, size), :], mine_ref, other_ref, mass_ref)
 
@@ -291,18 +295,16 @@
     held, turned, mine, other = pl.pallas_call(
         first_kernel,
         out_shape=(held_shape, turned_shape, sent_shape, sent_shape),
-        in_specs=[SMEM, VMEM, HBM, HBM],
+        in_specs=[SMEM, VMEM, HBM, VMEM],
         out_specs=(VMEM,) * 4,
         scratch_shapes=[
-            pltpu.VMEM((base_width, rows), f32),
             pltpu.VMEM((rows, anchors), f32),
             pltpu.SemaphoreType.DMA((pieces,)),
-            pltpu.SemaphoreType.DMA,
         ],
-        compiler_params=grant(23),
+        compiler_params=grant(8),
         cost_estimate=pl.CostEstimate(flops=8_000_000_000, bytes_accessed=40_000_000, transcendentals=base_width * rows),
         name="first_masses",
-    )(base_place, base_tokens, base_anchors, base)
+    )(base_place, base_tokens, pltpu.with_memory_space_constraint(base_anchors, pltpu.HBM), base)
 
     def both(mine, other, *more):
         other = lax.ppermute(other, "core", swap)
@@ -342,9 +344,14 @@
             no_update(kernel) if update is None else kernel,
             out_shape=update_shape if last else (update_shape, sent_shape, sent_shape),
             in_specs=[SMEM] + [VMEM] * (len(operands) - 1),
-            out_specs=VMEM if last else (VMEM, VMEM, VMEM),
-            scratch_shapes=[pltpu.VMEM((rows, anchors), bf16)]
-            + ([] if last else [pltpu.VMEM((base_width, rows), f32), pltpu.VMEM((rows, anchors), f32)]),
+            out_specs=HBM if last else (VMEM, VMEM, VMEM),
+            scratch_shapes=([pltpu.VMEM((base_width, rows), f32)] if last else [])
+            + [pltpu.VMEM((rows, anchors), bf16)]
+            + (
+                [pltpu.SemaphoreType.DMA((pieces,))]
+                if last
+                else [pltpu.VMEM((base_width, rows), f32), pltpu.VMEM((rows, anchors), f32)]
+            ),
             compiler_params=grant(7),
             name="step",
         )(*operands)

time: 146 us -> 142 us (0.973)
  Pallas kernels: 34.6 us -> 31.1 us
    pallas_call x1, Pallas kernels: 12.3 us -> 9.48 us  [shards(): pl.pallas_call(first_kernel, out_shape=(held_shape, turned_shape, sent_sh...]
where the time goes in v3:
time: 142 us; the launch traced here: 141 us
  blocking collectives  72 us (51%)
  Pallas kernels  31.1 us (22%)
  waiting for transfers between devices  19.9 us (14%)
  starting transfers between devices  17.9 us (13%)
    all_to_all x3, blocking collectives, shards(): got = lax.all_to_all(sent, CHIPS[1:], 0, 0, tiled=True)  38.8 us
    all_to_all x3, blocking collectives, shards(): gaps = lax.all_to_all(copies, CHIPS[1:], 0, 0, tiled=True)  33.2 us
    pallas_call x3, Pallas kernels, shards(): pl.pallas_call(no_update(kernel) if update is None else kernel, out_shape...  16.7 us
    ppermute x3, waiting for transfers between devices, shards(): targets[far] = lax.ppermute(targets[far], 'rows', ring)  11.1 us
    pallas_call x1, Pallas kernels, shards(): pl.pallas_call(first_kernel, out_shape=(held_shape, turned_shape, sent_sh...  9.48 us
    ppermute x3, starting transfers between devices, shards(): other_gaps = lax.ppermute(gaps, 'core', swap)  9.41 us
    ppermute x3, starting transfers between devices, shards(): targets[far] = lax.ppermute(targets[far], 'rows', ring)  5.79 us
    ppermute x3, waiting for transfers between devices, shards(): other_gaps = lax.ppermute(gaps, 'core', swap)  3.63 us
  transfers between devices with their start and end apart: 11, of which 8 were waited for; matrix products, arithmetic and copies ran while one was open for 0% of the time, Pallas kernels for 0%

profile of v3, /device:TPU:1, one launch (start us, length us, event | category | flops | bytes accessed | tf_op | source)
XLA Modules:
  0.0 141.4 jit_solution(1990527517605278758)
XLA Ops:
  0.0 0.0 copy-start.2
  0.0 0.0 copy-start
  0.0 1.4 collective-permute-start.1
  1.4 0.0 collective-permute-start
  1.4 0.1 pad_add_fusion.place_ref
  1.5 0.1 pad_add_fusion.1.place_ref
  1.5 2.7 %collective-permute-done.rest_3_ = bf16[512,250]{1,0:T(8,128)(2,1)S(1)} collective-permute-done((bf16[512,250]{1,0:T(8,128)(2,1)}, bf16[512,250]{1,0:T(8,128)(2,1)S(1)}, u32[]{:S(2)}, u32[]{:S(2)}) %collective-permute-start) | collective-permute-done | bytes 256032 | tf_op jit(solution)/shard_map/ppermute | solution.py:267
  4.3 0.0 collective-permute-done.1.rest_4_
  4.3 3.2 %target_parts.1 = (bf16[128,1024]{1,0:T(8,128)(2,1)S(1)}, bf16[128,1024]{1,0:T(8,128)(2,1)S(1)}, bf16[128,1024]{1,0:T(8,128)(2,1)S(1)}, bf16[128,1024]{1,0:T(8,128)(2,1)S(1)}) custom-call(s32[4]{0:T(128)S(1)} %pad_add_fusion.1.place_ref, s32[1,2048]{1,0:T(1,128)} %bitcast.18, bf16[512,250]{1,0:T(8,128)(2,1)} %rest_1_.1, bf16[250,2048]{1,0:T(8,128)(2,1)} %rest_2_.1, ...), custom_call_target="tpu_custom_call" | custom-call | tf_op jit(solution)/shard_map/target_parts/pallas_call | solution.py:270
  7.4 0.0 copy-done.2
  7.5 0.0 copy-done
  7.5 9.5 %first_masses.1 = (bf16[4008,2048]{1,0:T(8,128)(2,1)S(1)}, bf16[2048,4096]{1,0:T(8,128)(2,1)S(1)}, bf16[16,8,1152]{2,1,0:T(8,128)(2,1)S(1)}, bf16[16,8,1152]{2,1,0:T(8,128)(2,1)S(1)}) custom-call(s32[2]{0:T(128)S(1)} %pad_add_fusion.place_ref, s32[1,2048]{1,0:T(1,128)S(1)} %bitcast.17, bf16[4008,2048]{1,0:T(8,128)(2,1)} %anchors_ref.1, f32[4008,128]{1,0:T(8,128)S(1)} %bitcast.10), custom_call_target="tpu_custom_call" | custom-call | flops 8000000000 | bytes 40000000 | tf_op jit(solution)/shard_map/first_masses/pallas_call | solution.py:295
  16.9 0.5 collective-permute-start.2
  17.4 1.8 %collective-permute-start.3 = (bf16[128,1024]{1,0:T(8,128)(2,1)S(1)}, bf16[128,1024]{1,0:T(8,128)(2,1)S(1)}, u32[]{:S(2)}, u32[]{:S(2)}) collective-permute-start(bf16[128,1024]{1,0:T(8,128)(2,1)S(1)} %get-tuple-element.36), channel_id=1, source_target_pairs={{0,32},{32,64},{64,96},{96,0},{1,33},{33,65},{65,97},{97,1},{2,34}... | collective-permute-start | bytes 786440 | tf_op jit(solution)/shard_map/ppermute | solution.py:289
  19.2 3.3 %collective-permute-start.4 = (bf16[128,1024]{1,0:T(8,128)(2,1)S(1)}, bf16[128,1024]{1,0:T(8,128)(2,1)S(1)}, u32[]{:S(2)}, u32[]{:S(2)}) collective-permute-start(bf16[128,1024]{1,0:T(8,128)(2,1)S(1)} %get-tuple-element.37), channel_id=1, source_target_pairs={{0,64},{32,96},{64,0},{96,32},{1,65},{33,97},{65,1},{97,33},{2,66}... | collective-permute-start | bytes 786440 | tf_op jit(solution)/shard_map/ppermute | solution.py:289
  22.5 0.7 collective-permute-start.5
  23.2 4.6 %collective-permute-done.3.rest_1_ = bf16[128,1024]{1,0:T(8,128)(2,1)S(1)} collective-permute-done((bf16[128,1024]{1,0:T(8,128)(2,1)S(1)}, bf16[128,1024]{1,0:T(8,128)(2,1)S(1)}, u32[]{:S(2)}, u32[]{:S(2)}) %collective-permute-start.3) | collective-permute-done | bytes 262176 | tf_op jit(solution)/shard_map/ppermute | solution.py:289
  27.8 6.5 %collective-permute-done.4.rest_2_ = bf16[128,1024]{1,0:T(8,128)(2,1)S(1)} collective-permute-done((bf16[128,1024]{1,0:T(8,128)(2,1)S(1)}, bf16[128,1024]{1,0:T(8,128)(2,1)S(1)}, u32[]{:S(2)}, u32[]{:S(2)}) %collective-permute-start.4) | collective-permute-done | bytes 262176 | tf_op jit(solution)/shard_map/ppermute | solution.py:289
  34.3 0.0 collective-permute-done.5.rest_3_
  34.3 0.0 collective-permute-done.2.other_ref
  34.3 0.0 copy-start.1
  34.3 0.5 pair.3
  34.8 17.0 %all_to_all.30.in_ref = bf16[16,8,2176]{2,1,0:T(8,128)(2,1)S(1)} all-to-all(bf16[16,8,2176]{2,1,0:T(8,128)(2,1)S(1)} %pair.3), channel_id=1, replica_groups=mesh['rows'=4,'x'=4,'y'=4,'core'=2] {'x','y'}, dimensions={0} | all-to-all | bytes 1114112 | tf_op jit(solution)/shard_map/all_to_all | solution.py:324
  51.8 0.3 owner.3
  52.1 10.8 %all_to_all.31.mine_gap_ref = bf16[16,8,1152]{2,1,0:T(8,128)(2,1)S(1)} all-to-all(bf16[16,8,1152]{2,1,0:T(8,128)(2,1)S(1)} %get-tuple-element.39), channel_id=1, replica_groups=mesh['rows'=4,'x'=4,'y'=4,'core'=2] {'x','y'}, dimensions={0} | all-to-all | bytes 589824 | tf_op jit(solution)/shard_map/all_to_all | solution.py:339
  62.8 3.6 %collective-permute-start.6 = (bf16[16,8,1152]{2,1,0:T(8,128)(2,1)S(1)}, bf16[16,8,1152]{2,1,0:T(8,128)(2,1)S(1)}, u32[]{:S(2)}, u32[]{:S(2)}) collective-permute-start(bf16[16,8,1152]{2,1,0:T(8,128)(2,1)S(1)} %all_to_all.31.mine_gap_ref), channel_id=1, source_target_pairs={{0,1},{1,0},{2,3},{3,2},{4,5},{5,4},{6,7},{7,6},{8,9},{9,8},{10,11... | collective-permute-start | bytes 884744 | tf_op jit(solution)/shard_map/ppermute | solution.py:340
  66.4 1.2 collective-permute-done.6.other_gap_ref
  67.6 0.0 copy-done.1
  67.6 6.1 %step.3 = (f32[4008,128]{1,0:T(8,128)S(1)}, bf16[16,8,1152]{2,1,0:T(8,128)(2,1)S(1)}, bf16[16,8,1152]{2,1,0:T(8,128)(2,1)S(1)}) custom-call(s32[2]{0:T(128)S(1)} %pad_add_fusion.place_ref, bf16[16,8,1152]{2,1,0:T(8,128)(2,1)S(1)} %all_to_all.31.mine_gap_ref, bf16[16,8,1152]{2,1,0:T(8,128)(2,1)S(1)} %collective-permute-done.6.other_gap_ref, ...), custom_call_target="tpu_custom_call" | custom-call | tf_op jit(solution)/shard_map/step/pallas_call | solution.py:343
  73.8 0.4 collective-permute-start.7
  74.2 1.2 collective-permute-done.7.other_ref
  75.4 0.3 pair.4
  75.7 10.9 %all_to_all.32.in_ref = bf16[16,8,1152]{2,1,0:T(8,128)(2,1)S(1)} all-to-all(bf16[16,8,1152]{2,1,0:T(8,128)(2,1)S(1)} %pair.4), channel_id=1, replica_groups=mesh['rows'=4,'x'=4,'y'=4,'core'=2] {'x','y'}, dimensions={0} | all-to-all | bytes 589824 | tf_op jit(solution)/shard_map/all_to_all | solution.py:324
  86.6 0.3 owner.4
  86.9 11.2 %all_to_all.33.mine_gap_ref = bf16[16,8,1152]{2,1,0:T(8,128)(2,1)S(1)} all-to-all(bf16[16,8,1152]{2,1,0:T(8,128)(2,1)S(1)} %owner.4), channel_id=1, replica_groups=mesh['rows'=4,'x'=4,'y'=4,'core'=2] {'x','y'}, dimensions={0} | all-to-all | bytes 589824 | tf_op jit(solution)/shard_map/all_to_all | solution.py:339
  98.1 2.9 %collective-permute-start.8 = (bf16[16,8,1152]{2,1,0:T(8,128)(2,1)S(1)}, bf16[16,8,1152]{2,1,0:T(8,128)(2,1)S(1)}, u32[]{:S(2)}, u32[]{:S(2)}) collective-permute-start(bf16[16,8,1152]{2,1,0:T(8,128)(2,1)S(1)} %all_to_all.33.mine_gap_ref), channel_id=1, source_target_pairs={{0,1},{1,0},{2,3},{3,2},{4,5},{5,4},{6,7},{7,6},{8,9},{9,8},{10,11... | collective-permute-start | bytes 884744 | tf_op jit(solution)/shard_map/ppermute | solution.py:340
  101.0 1.2 collective-permute-done.8.other_gap_ref
  102.2 6.3 %step.4 = (f32[4008,128]{1,0:T(8,128)S(1)}, bf16[16,8,1152]{2,1,0:T(8,128)(2,1)S(1)}, bf16[16,8,1152]{2,1,0:T(8,128)(2,1)S(1)}) custom-call(s32[2]{0:T(128)S(1)} %pad_add_fusion.place_ref, bf16[16,8,1152]{2,1,0:T(8,128)(2,1)S(1)} %all_to_all.33.mine_gap_ref, bf16[16,8,1152]{2,1,0:T(8,128)(2,1)S(1)} %collective-permute-done.8.other_gap_ref, ...), custom_call_target="tpu_custom_call" | custom-call | tf_op jit(solution)/shard_map/step/pallas_call | solution.py:343
  108.5 0.4 collective-permute-start.9
  108.9 1.2 collective-permute-done.9.other_ref
  110.2 0.3 pair.5
  110.4 10.9 %all_to_all.34.in_ref = bf16[16,8,1152]{2,1,0:T(8,128)(2,1)S(1)} all-to-all(bf16[16,8,1152]{2,1,0:T(8,128)(2,1)S(1)} %pair.5), channel_id=1, replica_groups=mesh['rows'=4,'x'=4,'y'=4,'core'=2] {'x','y'}, dimensions={0} | all-to-all | bytes 589824 | tf_op jit(solution)/shard_map/all_to_all | solution.py:324
  121.4 0.3 owner.5
  121.6 11.2 %all_to_all.35.mine_gap_ref = bf16[16,8,1152]{2,1,0:T(8,128)(2,1)S(1)} all-to-all(bf16[16,8,1152]{2,1,0:T(8,128)(2,1)S(1)} %owner.5), channel_id=1, replica_groups=mesh['rows'=4,'x'=4,'y'=4,'core'=2] {'x','y'}, dimensions={0} | all-to-all | bytes 589824 | tf_op jit(solution)/shard_map/all_to_all | solution.py:339
  132.9 2.9 %collective-permute-start.10 = (bf16[16,8,1152]{2,1,0:T(8,128)(2,1)S(1)}, bf16[16,8,1152]{2,1,0:T(8,128)(2,1)S(1)}, u32[]{:S(2)}, u32[]{:S(2)}) collective-permute-start(bf16[16,8,1152]{2,1,0:T(8,128)(2,1)S(1)} %all_to_all.35.mine_gap_ref), channel_id=1, source_target_pairs={{0,1},{1,0},{2,3},{3,2},{4,5},{5,4},{6,7},{7,6},{8,9},{9,8},{10,11... | collective-permute-start | bytes 884744 | tf_op jit(solution)/shard_map/ppermute | solution.py:340
  135.8 1.2 collective-permute-done.10.other_gap_ref
  137.0 4.3 %step.5 = f32[4008,128]{1,0:T(8,128)} custom-call(s32[2]{0:T(128)S(1)} %pad_add_fusion.place_ref, bf16[16,8,1152]{2,1,0:T(8,128)(2,1)S(1)} %all_to_all.35.mine_gap_ref, bf16[16,8,1152]{2,1,0:T(8,128)(2,1)S(1)} %collective-permute-done.10.other_gap_ref, s32[1,128]{1,0:T(1,128)S(1)} %bitcast.16, f32[4008,128]{1,0:T(8,128)S(1)} %bitcast.13, ...), custom_call_target="tpu_custom_call" | custom-call | tf_op jit(solution)/shard_map/step/pallas_call | solution.py:343
Async XLA Ops:
  0.0 7.4 %copy-start.2 = (s32[2048]{0:T(1024)S(1)}, s32[2048]{0:T(1024)}, u32[]{:S(2)}) copy-start(s32[2048]{0:T(1024)} %param.12) | copy-start | bytes 24580
  0.0 7.5 %copy-start = (f32[128,4008]{0,1:T(8,128)S(1)}, f32[128,4008]{0,1:T(8,128)}, u32[]{:S(2)}) copy-start(f32[128,4008]{0,1:T(8,128)} %param.10) | copy-start | bytes 6156292
  0.0 4.3 %collective-permute-start.1 = (bf16[250,2048]{1,0:T(8,128)(2,1)}, bf16[250,2048]{1,0:T(8,128)(2,1)S(1)}, u32[]{:S(2)}, u32[]{:S(2)}) collective-permute-start(bf16[250,2048]{1,0:T(8,128)(2,1)} %rest_2_.1), channel_id=1, source_target_pairs={{0,1},{1,0},{2,3},{3,2},{4,5},{5,4},{6,7},{7,6},{8,9},{9,8},{10,11... | collective-permute-start | bytes 3072008 | tf_op jit(solution)/shard_map/ppermute | solution.py:268
  1.4 2.9 %collective-permute-start = (bf16[512,250]{1,0:T(8,128)(2,1)}, bf16[512,250]{1,0:T(8,128)(2,1)S(1)}, u32[]{:S(2)}, u32[]{:S(2)}) collective-permute-start(bf16[512,250]{1,0:T(8,128)(2,1)} %rest_1_.1), channel_id=1, source_target_pairs={{0,1},{1,0},{2,3},{3,2},{4,5},{5,4},{6,7},{7,6},{8,9},{9,8},{10,11... | collective-permute-start | bytes 768008 | tf_op jit(solution)/shard_map/ppermute | solution.py:267
  16.9 17.4 %collective-permute-start.2 = (bf16[16,8,1152]{2,1,0:T(8,128)(2,1)S(1)}, bf16[16,8,1152]{2,1,0:T(8,128)(2,1)S(1)}, u32[]{:S(2)}, u32[]{:S(2)}) collective-permute-start(bf16[16,8,1152]{2,1,0:T(8,128)(2,1)S(1)} %get-tuple-element.34), channel_id=1, source_target_pairs={{0,1},{1,0},{2,3},{3,2},{4,5},{5,4},{6,7},{7,6},{8,9},{9,8},{10,11... | collective-permute-start | bytes 884744 | tf_op jit(solution)/shard_map/ppermute | solution.py:310
  17.4 10.4 %collective-permute-start.3 = (bf16[128,1024]{1,0:T(8,128)(2,1)S(1)}, bf16[128,1024]{1,0:T(8,128)(2,1)S(1)}, u32[]{:S(2)}, u32[]{:S(2)}) collective-permute-start(bf16[128,1024]{1,0:T(8,128)(2,1)S(1)} %get-tuple-element.36), channel_id=1, source_target_pairs={{0,32},{32,64},{64,96},{96,0},{1,33},{33,65},{65,97},{97,1},{2,34}... | collective-permute-start | bytes 786440 | tf_op jit(solution)/shard_map/ppermute | solution.py:289
  19.2 15.2 %collective-permute-start.4 = (bf16[128,1024]{1,0:T(8,128)(2,1)S(1)}, bf16[128,1024]{1,0:T(8,128)(2,1)S(1)}, u32[]{:S(2)}, u32[]{:S(2)}) collective-permute-start(bf16[128,1024]{1,0:T(8,128)(2,1)S(1)} %get-tuple-element.37), channel_id=1, source_target_pairs={{0,64},{32,96},{64,0},{96,32},{1,65},{33,97},{65,1},{97,33},{2,66}... | collective-permute-start | bytes 786440 | tf_op jit(solution)/shard_map/ppermute | solution.py:289
  22.5 11.9 %collective-permute-start.5 = (bf16[128,1024]{1,0:T(8,128)(2,1)S(1)}, bf16[128,1024]{1,0:T(8,128)(2,1)S(1)}, u32[]{:S(2)}, u32[]{:S(2)}) collective-permute-start(bf16[128,1024]{1,0:T(8,128)(2,1)S(1)} %get-tuple-element.38), channel_id=1, source_target_pairs={{0,96},{32,0},{64,32},{96,64},{1,97},{33,1},{65,33},{97,65},{2,98}... | collective-permute-start | bytes 786440 | tf_op jit(solution)/shard_map/ppermute | solution.py:289
  34.3 33.3 %copy-start.1 = (s32[128]{0:T(128)S(1)}, s32[128]{0:T(128)}, u32[]{:S(2)}) copy-start(s32[128]{0:T(128)} %param.13) | copy-start | bytes 1540
  62.8 4.8 %collective-permute-start.6 = (bf16[16,8,1152]{2,1,0:T(8,128)(2,1)S(1)}, bf16[16,8,1152]{2,1,0:T(8,128)(2,1)S(1)}, u32[]{:S(2)}, u32[]{:S(2)}) collective-permute-start(bf16[16,8,1152]{2,1,0:T(8,128)(2,1)S(1)} %all_to_all.31.mine_gap_ref), channel_id=1, source_target_pairs={{0,1},{1,0},{2,3},{3,2},{4,5},{5,4},{6,7},{7,6},{8,9},{9,8},{10,11... | collective-permute-start | bytes 884744 | tf_op jit(solution)/shard_map/ppermute | solution.py:340
  73.8 1.7 %collective-permute-start.7 = (bf16[16,8,1152]{2,1,0:T(8,128)(2,1)S(1)}, bf16[16,8,1152]{2,1,0:T(8,128)(2,1)S(1)}, u32[]{:S(2)}, u32[]{:S(2)}) collective-permute-start(bf16[16,8,1152]{2,1,0:T(8,128)(2,1)S(1)} %get-tuple-element.43), channel_id=1, source_target_pairs={{0,1},{1,0},{2,3},{3,2},{4,5},{5,4},{6,7},{7,6},{8,9},{9,8},{10,11... | collective-permute-start | bytes 884744 | tf_op jit(solution)/shard_map/ppermute | solution.py:310
  98.1 4.1 %collective-permute-start.8 = (bf16[16,8,1152]{2,1,0:T(8,128)(2,1)S(1)}, bf16[16,8,1152]{2,1,0:T(8,128)(2,1)S(1)}, u32[]{:S(2)}, u32[]{:S(2)}) collective-permute-start(bf16[16,8,1152]{2,1,0:T(8,128)(2,1)S(1)} %all_to_all.33.mine_gap_ref), channel_id=1, source_target_pairs={{0,1},{1,0},{2,3},{3,2},{4,5},{5,4},{6,7},{7,6},{8,9},{9,8},{10,11... | collective-permute-start | bytes 884744 | tf_op jit(solution)/shard_map/ppermute | solution.py:340
  108.5 1.7 %collective-permute-start.9 = (bf16[16,8,1152]{2,1,0:T(8,128)(2,1)S(1)}, bf16[16,8,1152]{2,1,0:T(8,128)(2,1)S(1)}, u32[]{:S(2)}, u32[]{:S(2)}) collective-permute-start(bf16[16,8,1152]{2,1,0:T(8,128)(2,1)S(1)} %get-tuple-element.47), channel_id=1, source_target_pairs={{0,1},{1,0},{2,3},{3,2},{4,5},{5,4},{6,7},{7,6},{8,9},{9,8},{10,11... | collective-permute-start | bytes 884744 | tf_op jit(solution)/shard_map/ppermute | solution.py:310
  132.9 4.1 %collective-permute-start.10 = (bf16[16,8,1152]{2,1,0:T(8,128)(2,1)S(1)}, bf16[16,8,1152]{2,1,0:T(8,128)(2,1)S(1)}, u32[]{:S(2)}, u32[]{:S(2)}) collective-permute-start(bf16[16,8,1152]{2,1,0:T(8,128)(2,1)S(1)} %all_to_all.35.mine_gap_ref), channel_id=1, source_target_pairs={{0,1},{1,0},{2,3},{3,2},{4,5},{5,4},{6,7},{7,6},{8,9},{9,8},{10,11... | collective-permute-start | bytes 884744 | tf_op jit(solution)/shard_map/ppermute | solution.py:340

commit v4 on v3

--- a/solution.py
+++ b/solution.py
@@ -72,6 +72,44 @@
         columns = pl.ds(pl.multiple_of(which * half, half), half)
         out_ref[:, :, :half] = mass_ref[:, columns].reshape(groups, eight, half).astype(jnp.bfloat16)
         out_ref[:, :, half:] = stats
+
+
+def put_other(core, logits_ref, held_ref, other_ref, weights_ref, mass_ref):
+    extent, rows = logits_ref.shape
+    groups, eight, width = other_ref.shape
+    half = width - LANES
+    columns = pl.ds(pl.multiple_of((1 - core) * half, half), half)
+    top = jnp.max(logits_ref[...], axis=0, keepdims=True)
+    total = jnp.zeros((1, rows), jnp.float32)
+    for start, size in chunks_of(extent):
+        weights = jnp.exp(logits_ref[pl.ds(start, size), :] - top)
+        total = total + jnp.sum(weights, axis=0, keepdims=True)
+        turned = weights.T.astype(jnp.bfloat16)
+        weights_ref[:, start : start + size] = turned
+        part = jnp.dot(turned, held_ref[pl.ds(start, size), columns], preferred_element_type=jnp.float32)
+        if start == 0:
+            mass_ref[...] = part
+        else:
+            mass_ref[...] += part
+    parts = three_parts(top) + three_parts(total)
+    stats = jnp.concatenate(list(parts) + [jnp.zeros((LANES - len(parts), rows), jnp.float32)], axis=0)
+    other_ref[:, :, :half] = mass_ref[...].reshape(groups, eight, half).astype(jnp.bfloat16)
+    other_ref[:, :, half:] = stats.T.reshape(groups, eight, LANES).astype(jnp.bfloat16)
+
+
+def mine_kernel(place_ref, weights_ref, held_ref, other_ref, turned_ref, mine_ref, mass_ref):
+    groups, eight, width = mine_ref.shape
+    half = width - LANES
+    columns = pl.ds(pl.multiple_of(place_ref[1] * half, half), half)
+    for start, size in chunks_of(held_ref.shape[0]):
+        block = held_ref[pl.ds(start, size), columns]
+        part = jnp.dot(weights_ref[:, start : start + size], block, preferred_element_type=jnp.float32)
+        if start == 0:
+            mass_ref[...] = part
+        else:
+            mass_ref[...] += part
+    mine_ref[:, :, :half] = mass_ref[...].reshape(groups, eight, half).astype(jnp.bfloat16)
+    mine_ref[:, :, half:] = other_ref[:, :, half:]
 
 
 def first_kernel(place_ref, tokens_ref, anchors_ref, logits_ref, held_ref, turned_ref, mine_ref, other_ref, mass_ref, sems):
@@ -163,7 +201,7 @@
     if last:
         out_ref, new_ref, gap_all, sems = rest
     else:
-        held_ref, new_ref, mine_ref, other_ref, gap_all, logits_ref, mass_ref = rest
+        held_ref, new_ref, weights_ref, other_ref, gap_all, logits_ref, mass_ref = rest
     extent, rows = base_ref.shape
     half = mine_gap_ref.shape[2] - LANES
     core = place_ref[1]
@@ -203,7 +241,7 @@
     for copy in copies:
         copy.wait()
     if not last:
-        put_masses(core, logits_ref, lambda start, size: held_ref[pl.ds(start, size), :], mine_ref, other_ref, mass_ref)
+        put_other(core, logits_ref, held_ref, other_ref, weights_ref, mass_ref)
 
 
 def no_update(kernel):
@@ -275,7 +313,7 @@
         scratch_shapes=[pltpu.VMEM(small_tokens.shape, jnp.int32)]
         + [pltpu.VMEM(each.shape, bf16) for each in (expert_delta, small_anchors)] * 2
         + [pltpu.VMEM((all_rows, half), f32), pltpu.SemaphoreType.DMA((5,))],
-        compiler_params=grant(20),
+        compiler_params=grant(14),
         name="target_parts",
     )(
         small_place,
@@ -291,6 +329,7 @@
     sent_shape = jax.ShapeDtypeStruct((groups, eight, width), bf16)
     held_shape = pltpu.VMEM((base_width, anchors), bf16)
     turned_shape = pltpu.VMEM((anchors, -(-base_width // LANES) * LANES), bf16)
+    weights_shape = jax.ShapeDtypeStruct((rows, -(-base_width // LANES) * LANES), bf16)
     update_shape = jax.ShapeDtypeStruct((base_width, rows), f32)
     held, turned, mine, other = pl.pallas_call(
         first_kernel,
@@ -301,7 +340,7 @@
             pltpu.VMEM((rows, anchors), f32),
             pltpu.SemaphoreType.DMA((pieces,)),
         ],
-        compiler_params=grant(8),
+        compiler_params=grant(4),
         cost_estimate=pl.CostEstimate(flops=8_000_000_000, bytes_accessed=40_000_000, transcendentals=base_width * rows),
         name="first_masses",
     )(base_place, base_tokens, pltpu.with_memory_space_constraint(base_anchors, pltpu.HBM), base)
@@ -313,7 +352,7 @@
             out_shape=jax.ShapeDtypeStruct((groups, eight, width + (half if more else 0)), bf16),
             in_specs=[VMEM] * (2 + len(more)),
             out_specs=VMEM,
-            compiler_params=grant(5),
+            compiler_params=grant(2),
             name="pair",
         )(mine, other, *more)
 
@@ -329,7 +368,7 @@
             out_shape=(sent_shape, target_shape) if first else sent_shape,
             in_specs=[VMEM] if first else [VMEM, VMEM],
             out_specs=(VMEM, VMEM) if first else VMEM,
-            compiler_params=grant(4),
+            compiler_params=grant(2),
             name="owner",
         )(*((got,) if first else (got, target)))
         if first:
@@ -342,7 +381,7 @@
         operands = [base_place, gaps, other_gaps, active, base] + ([] if update is None else [update]) + [turned] + ([] if last else [held])
         result = pl.pallas_call(
             no_update(kernel) if update is None else kernel,
-            out_shape=update_shape if last else (update_shape, sent_shape, sent_shape),
+            out_shape=update_shape if last else (update_shape, weights_shape, sent_shape),
             in_specs=[SMEM] + [VMEM] * (len(operands) - 1),
             out_specs=HBM if last else (VMEM, VMEM, VMEM),
             scratch_shapes=([pltpu.VMEM((base_width, rows), f32)] if last else [])
@@ -350,15 +389,24 @@
             + (
                 [pltpu.SemaphoreType.DMA((pieces,))]
                 if last
-                else [pltpu.VMEM((base_width, rows), f32), pltpu.VMEM((rows, anchors), f32)]
+                else [pltpu.VMEM((base_width, rows), f32), pltpu.VMEM((rows, half), f32)]
             ),
-            compiler_params=grant(7),
+            compiler_params=grant(5),
             name="step",
         )(*operands)
         if last:
             update = result
         else:
-            update, mine, other = result
+            update, weights, other = result
+            mine = pl.pallas_call(
+                mine_kernel,
+                out_shape=sent_shape,
+                in_specs=[SMEM, VMEM, VMEM, VMEM, HBM],
+                out_specs=VMEM,
+                scratch_shapes=[pltpu.VMEM((rows, half), f32)],
+                compiler_params=grant(2),
+                name="own_half",
+            )(base_place, weights, held, other, turned)
             sent = both(mine, other)
     return update.T
 

time: 142 us -> 141 us (level)
  waiting for transfers between devices: 19.9 us -> 17.5 us
  Pallas kernels: 31.1 us -> 32.6 us
    pallas_call x0 -> x2, Pallas kernels: none -> 3.6 us  [shards(): pl.pallas_call(mine_kernel, out_shape=sent_shape, in_specs=[SMEM, VMEM, V...]
    ppermute x3, waiting for transfers between devices: 2.46 us -> 0.01 us  [both(): other = lax.ppermute(other, 'core', swap)]
    pallas_call x3, Pallas kernels: 16.7 us -> 14.6 us  [shards(): pl.pallas_call(no_update(kernel) if update is None else kernel, out_shape...]
  transfers between devices with their start and end apart: 11 -> 11, of which waited for: 8 -> 6; matrix products, arithmetic and copies ran while one was open for 0% -> 0% of each run, Pallas kernels for 0% -> 3%
where the time goes in v4:
time: 141 us
  blocking collectives  72.6 us (51%)
  Pallas kernels  32.6 us (23%)
  starting transfers between devices  17.7 us (13%)
  waiting for transfers between devices  17.5 us (12%)
    all_to_all x3, blocking collectives, shards(): got = lax.all_to_all(sent, CHIPS[1:], 0, 0, tiled=True)  39.2 us
    all_to_all x3, blocking collectives, shards(): gaps = lax.all_to_all(copies, CHIPS[1:], 0, 0, tiled=True)  33.3 us
    pallas_call x3, Pallas kernels, shards(): pl.pallas_call(no_update(kernel) if update is None else kernel, out_shape...  14.6 us
    ppermute x3, waiting for transfers between devices, shards(): targets[far] = lax.ppermute(targets[far], 'rows', ring)  11.1 us
    pallas_call x1, Pallas kernels, shards(): pl.pallas_call(first_kernel, out_shape=(held_shape, turned_shape, sent_sh...  9.5 us
    ppermute x3, starting transfers between devices, shards(): other_gaps = lax.ppermute(gaps, 'core', swap)  8.92 us
    ppermute x3, starting transfers between devices, shards(): targets[far] = lax.ppermute(targets[far], 'rows', ring)  5.77 us
    ppermute x3, waiting for transfers between devices, shards(): other_gaps = lax.ppermute(gaps, 'core', swap)  3.63 us
  transfers between devices with their start and end apart: 11, of which 6 were waited for; matrix products, arithmetic and copies ran while one was open for 0% of the time, Pallas kernels for 3%

profile of v4, /device:TPU:1, one launch (start us, length us, event | category | flops | bytes accessed | tf_op | source)
XLA Modules:
  0.0 140.9 jit_solution(14402955728697885522)
XLA Ops:
  0.0 0.0 copy-start.2
  0.0 0.0 copy-start
  0.0 1.4 collective-permute-start.1
  1.4 0.0 collective-permute-start
  1.4 0.1 pad_add_fusion.place_ref
  1.5 0.1 pad_add_fusion.1.place_ref
  1.5 2.7 %collective-permute-done.rest_3_ = bf16[512,250]{1,0:T(8,128)(2,1)S(1)} collective-permute-done((bf16[512,250]{1,0:T(8,128)(2,1)}, bf16[512,250]{1,0:T(8,128)(2,1)S(1)}, u32[]{:S(2)}, u32[]{:S(2)}) %collective-permute-start) | collective-permute-done | bytes 256032 | tf_op jit(solution)/shard_map/ppermute | solution.py:305
  4.3 0.0 collective-permute-done.1.rest_4_
  4.3 3.2 %target_parts.1 = (bf16[128,1024]{1,0:T(8,128)(2,1)S(1)}, bf16[128,1024]{1,0:T(8,128)(2,1)S(1)}, bf16[128,1024]{1,0:T(8,128)(2,1)S(1)}, bf16[128,1024]{1,0:T(8,128)(2,1)S(1)}) custom-call(s32[4]{0:T(128)S(1)} %pad_add_fusion.1.place_ref, s32[1,2048]{1,0:T(1,128)} %bitcast.18, bf16[512,250]{1,0:T(8,128)(2,1)} %rest_1_.1, bf16[250,2048]{1,0:T(8,128)(2,1)} %rest_2_.1, ...), custom_call_target="tpu_custom_call" | custom-call | tf_op jit(solution)/shard_map/target_parts/pallas_call | solution.py:308
  7.4 0.0 copy-done.2
  7.5 0.0 copy-done
  7.5 9.5 %first_masses.1 = (bf16[4008,2048]{1,0:T(8,128)(2,1)S(1)}, bf16[2048,4096]{1,0:T(8,128)(2,1)S(1)}, bf16[16,8,1152]{2,1,0:T(8,128)(2,1)S(1)}, bf16[16,8,1152]{2,1,0:T(8,128)(2,1)S(1)}) custom-call(s32[2]{0:T(128)S(1)} %pad_add_fusion.place_ref, s32[1,2048]{1,0:T(1,128)S(1)} %bitcast.17, bf16[4008,2048]{1,0:T(8,128)(2,1)} %anchors_ref.1, f32[4008,128]{1,0:T(8,128)S(1)} %bitcast.10), custom_call_target="tpu_custom_call" | custom-call | flops 8000000000 | bytes 40000000 | tf_op jit(solution)/shard_map/first_masses/pallas_call | solution.py:334
  17.0 0.5 collective-permute-start.2
  17.4 1.7 %collective-permute-start.3 = (bf16[128,1024]{1,0:T(8,128)(2,1)S(1)}, bf16[128,1024]{1,0:T(8,128)(2,1)S(1)}, u32[]{:S(2)}, u32[]{:S(2)}) collective-permute-start(bf16[128,1024]{1,0:T(8,128)(2,1)S(1)} %get-tuple-element.36), channel_id=1, source_target_pairs={{0,32},{32,64},{64,96},{96,0},{1,33},{33,65},{65,97},{97,1},{2,34}... | collective-permute-start | bytes 786440 | tf_op jit(solution)/shard_map/ppermute | solution.py:327
  19.2 3.3 %collective-permute-start.4 = (bf16[128,1024]{1,0:T(8,128)(2,1)S(1)}, bf16[128,1024]{1,0:T(8,128)(2,1)S(1)}, u32[]{:S(2)}, u32[]{:S(2)}) collective-permute-start(bf16[128,1024]{1,0:T(8,128)(2,1)S(1)} %get-tuple-element.37), channel_id=1, source_target_pairs={{0,64},{32,96},{64,0},{96,32},{1,65},{33,97},{65,1},{97,33},{2,66}... | collective-permute-start | bytes 786440 | tf_op jit(solution)/shard_map/ppermute | solution.py:327
  22.5 0.7 collective-permute-start.5
  23.2 4.6 %collective-permute-done.3.rest_1_ = bf16[128,1024]{1,0:T(8,128)(2,1)S(1)} collective-permute-done((bf16[128,1024]{1,0:T(8,128)(2,1)S(1)}, bf16[128,1024]{1,0:T(8,128)(2,1)S(1)}, u32[]{:S(2)}, u32[]{:S(2)}) %collective-permute-start.3) | collective-permute-done | bytes 262176 | tf_op jit(solution)/shard_map/ppermute | solution.py:327
  27.8 6.5 %collective-permute-done.4.rest_2_ = bf16[128,1024]{1,0:T(8,128)(2,1)S(1)} collective-permute-done((bf16[128,1024]{1,0:T(8,128)(2,1)S(1)}, bf16[128,1024]{1,0:T(8,128)(2,1)S(1)}, u32[]{:S(2)}, u32[]{:S(2)}) %collective-permute-start.4) | collective-permute-done | bytes 262176 | tf_op jit(solution)/shard_map/ppermute | solution.py:327
  34.4 0.0 collective-permute-done.5.rest_3_
  34.4 0.0 collective-permute-done.2.other_ref
  34.4 0.0 copy-start.1
  34.4 0.5 pair.3
  34.8 17.0 %all_to_all.30.in_ref = bf16[16,8,2176]{2,1,0:T(8,128)(2,1)S(1)} all-to-all(bf16[16,8,2176]{2,1,0:T(8,128)(2,1)S(1)} %pair.3), channel_id=1, replica_groups=mesh['rows'=4,'x'=4,'y'=4,'core'=2] {'x','y'}, dimensions={0} | all-to-all | bytes 1114112 | tf_op jit(solution)/shard_map/all_to_all | solution.py:363
  51.9 0.3 owner.3
  52.1 10.8 %all_to_all.31.mine_gap_ref = bf16[16,8,1152]{2,1,0:T(8,128)(2,1)S(1)} all-to-all(bf16[16,8,1152]{2,1,0:T(8,128)(2,1)S(1)} %get-tuple-element.39), channel_id=1, replica_groups=mesh['rows'=4,'x'=4,'y'=4,'core'=2] {'x','y'}, dimensions={0} | all-to-all | bytes 589824 | tf_op jit(solution)/shard_map/all_to_all | solution.py:378
  62.9 3.5 %collective-permute-start.6 = (bf16[16,8,1152]{2,1,0:T(8,128)(2,1)S(1)}, bf16[16,8,1152]{2,1,0:T(8,128)(2,1)S(1)}, u32[]{:S(2)}, u32[]{:S(2)}) collective-permute-start(bf16[16,8,1152]{2,1,0:T(8,128)(2,1)S(1)} %all_to_all.31.mine_gap_ref), channel_id=1, source_target_pairs={{0,1},{1,0},{2,3},{3,2},{4,5},{5,4},{6,7},{7,6},{8,9},{9,8},{10,11... | collective-permute-start | bytes 884744 | tf_op jit(solution)/shard_map/ppermute | solution.py:379
  66.5 1.2 collective-permute-done.6.other_gap_ref
  67.7 0.0 copy-done.1
  67.7 5.1 %step.3 = (f32[4008,128]{1,0:T(8,128)S(1)}, bf16[128,4096]{1,0:T(8,128)(2,1)S(1)}, bf16[16,8,1152]{2,1,0:T(8,128)(2,1)S(1)}) custom-call(s32[2]{0:T(128)S(1)} %pad_add_fusion.place_ref, bf16[16,8,1152]{2,1,0:T(8,128)(2,1)S(1)} %all_to_all.31.mine_gap_ref, bf16[16,8,1152]{2,1,0:T(8,128)(2,1)S(1)} %collective-permute-done.6.other_gap_ref, ...), custom_call_target="tpu_custom_call" | custom-call | tf_op jit(solution)/shard_map/step/pallas_call | solution.py:382
  72.7 0.5 collective-permute-start.7
  73.2 1.8 %own_half.2.mine_ref = bf16[16,8,1152]{2,1,0:T(8,128)(2,1)S(1)} custom-call(s32[2]{0:T(128)S(1)} %pad_add_fusion.place_ref, bf16[128,4096]{1,0:T(8,128)(2,1)S(1)} %get-tuple-element.42.weights_ref, bf16[4008,2048]{1,0:T(8,128)(2,1)S(1)} %get-tuple-element.41.rest_0_.held_ref, bf16[16,8,1152]{2,1,0:T(8,128)(2,1)S(1)} %get-tuple-element.43.other_ref, ...), custom_call_target="tpu_custom_call" | custom-call | tf_op jit(solution)/shard_map/own_half/pallas_call | solution.py:401
  75.0 0.0 collective-permute-done.7.other_ref
  75.0 0.3 pair.4
  75.3 11.1 %all_to_all.32.in_ref = bf16[16,8,1152]{2,1,0:T(8,128)(2,1)S(1)} all-to-all(bf16[16,8,1152]{2,1,0:T(8,128)(2,1)S(1)} %pair.4), channel_id=1, replica_groups=mesh['rows'=4,'x'=4,'y'=4,'core'=2] {'x','y'}, dimensions={0} | all-to-all | bytes 589824 | tf_op jit(solution)/shard_map/all_to_all | solution.py:363
  86.4 0.3 owner.4
  86.7 11.3 %all_to_all.33.mine_gap_ref = bf16[16,8,1152]{2,1,0:T(8,128)(2,1)S(1)} all-to-all(bf16[16,8,1152]{2,1,0:T(8,128)(2,1)S(1)} %owner.4), channel_id=1, replica_groups=mesh['rows'=4,'x'=4,'y'=4,'core'=2] {'x','y'}, dimensions={0} | all-to-all | bytes 589824 | tf_op jit(solution)/shard_map/all_to_all | solution.py:378
  98.0 2.7 %collective-permute-start.8 = (bf16[16,8,1152]{2,1,0:T(8,128)(2,1)S(1)}, bf16[16,8,1152]{2,1,0:T(8,128)(2,1)S(1)}, u32[]{:S(2)}, u32[]{:S(2)}) collective-permute-start(bf16[16,8,1152]{2,1,0:T(8,128)(2,1)S(1)} %all_to_all.33.mine_gap_ref), channel_id=1, source_target_pairs={{0,1},{1,0},{2,3},{3,2},{4,5},{5,4},{6,7},{7,6},{8,9},{9,8},{10,11... | collective-permute-start | bytes 884744 | tf_op jit(solution)/shard_map/ppermute | solution.py:379
  100.6 1.2 collective-permute-done.8.other_gap_ref
  101.9 5.2 %step.4 = (f32[4008,128]{1,0:T(8,128)S(1)}, bf16[128,4096]{1,0:T(8,128)(2,1)S(1)}, bf16[16,8,1152]{2,1,0:T(8,128)(2,1)S(1)}) custom-call(s32[2]{0:T(128)S(1)} %pad_add_fusion.place_ref, bf16[16,8,1152]{2,1,0:T(8,128)(2,1)S(1)} %all_to_all.33.mine_gap_ref, bf16[16,8,1152]{2,1,0:T(8,128)(2,1)S(1)} %collective-permute-done.8.other_gap_ref, ...), custom_call_target="tpu_custom_call" | custom-call | tf_op jit(solution)/shard_map/step/pallas_call | solution.py:382
  107.1 0.7 collective-permute-start.9
  107.8 1.8 %own_half.3.mine_ref = bf16[16,8,1152]{2,1,0:T(8,128)(2,1)S(1)} custom-call(s32[2]{0:T(128)S(1)} %pad_add_fusion.place_ref, bf16[128,4096]{1,0:T(8,128)(2,1)S(1)} %get-tuple-element.46.weights_ref, bf16[4008,2048]{1,0:T(8,128)(2,1)S(1)} %get-tuple-element.41.rest_0_.held_ref, bf16[16,8,1152]{2,1,0:T(8,128)(2,1)S(1)} %get-tuple-element.47.other_ref, ...), custom_call_target="tpu_custom_call" | custom-call | tf_op jit(solution)/shard_map/own_half/pallas_call | solution.py:401
  109.6 0.0 collective-permute-done.9.other_ref
  109.6 0.3 pair.5
  109.9 11.1 %all_to_all.34.in_ref = bf16[16,8,1152]{2,1,0:T(8,128)(2,1)S(1)} all-to-all(bf16[16,8,1152]{2,1,0:T(8,128)(2,1)S(1)} %pair.5), channel_id=1, replica_groups=mesh['rows'=4,'x'=4,'y'=4,'core'=2] {'x','y'}, dimensions={0} | all-to-all | bytes 589824 | tf_op jit(solution)/shard_map/all_to_all | solution.py:363
  120.9 0.3 owner.5
  121.2 11.3 %all_to_all.35.mine_gap_ref = bf16[16,8,1152]{2,1,0:T(8,128)(2,1)S(1)} all-to-all(bf16[16,8,1152]{2,1,0:T(8,128)(2,1)S(1)} %owner.5), channel_id=1, replica_groups=mesh['rows'=4,'x'=4,'y'=4,'core'=2] {'x','y'}, dimensions={0} | all-to-all | bytes 589824 | tf_op jit(solution)/shard_map/all_to_all | solution.py:378
  132.5 2.7 %collective-permute-start.10 = (bf16[16,8,1152]{2,1,0:T(8,128)(2,1)S(1)}, bf16[16,8,1152]{2,1,0:T(8,128)(2,1)S(1)}, u32[]{:S(2)}, u32[]{:S(2)}) collective-permute-start(bf16[16,8,1152]{2,1,0:T(8,128)(2,1)S(1)} %all_to_all.35.mine_gap_ref), channel_id=1, source_target_pairs={{0,1},{1,0},{2,3},{3,2},{4,5},{5,4},{6,7},{7,6},{8,9},{9,8},{10,11... | collective-permute-start | bytes 884744 | tf_op jit(solution)/shard_map/ppermute | solution.py:379
  135.2 1.2 collective-permute-done.10.other_gap_ref
  136.4 4.3 %step.5 = f32[4008,128]{1,0:T(8,128)} custom-call(s32[2]{0:T(128)S(1)} %pad_add_fusion.place_ref, bf16[16,8,1152]{2,1,0:T(8,128)(2,1)S(1)} %all_to_all.35.mine_gap_ref, bf16[16,8,1152]{2,1,0:T(8,128)(2,1)S(1)} %collective-permute-done.10.other_gap_ref, s32[1,128]{1,0:T(1,128)S(1)} %bitcast.16, f32[4008,128]{1,0:T(8,128)S(1)} %bitcast.13, ...), custom_call_target="tpu_custom_call" | custom-call | tf_op jit(solution)/shard_map/step/pallas_call | solution.py:382
Async XLA Ops:
  0.0 7.4 %copy-start.2 = (s32[2048]{0:T(1024)S(1)}, s32[2048]{0:T(1024)}, u32[]{:S(2)}) copy-start(s32[2048]{0:T(1024)} %param.12) | copy-start | bytes 24580
  0.0 7.5 %copy-start = (f32[128,4008]{0,1:T(8,128)S(1)}, f32[128,4008]{0,1:T(8,128)}, u32[]{:S(2)}) copy-start(f32[128,4008]{0,1:T(8,128)} %param.10) | copy-start | bytes 6156292
  0.0 4.3 %collective-permute-start.1 = (bf16[250,2048]{1,0:T(8,128)(2,1)}, bf16[250,2048]{1,0:T(8,128)(2,1)S(1)}, u32[]{:S(2)}, u32[]{:S(2)}) collective-permute-start(bf16[250,2048]{1,0:T(8,128)(2,1)} %rest_2_.1), channel_id=1, source_target_pairs={{0,1},{1,0},{2,3},{3,2},{4,5},{5,4},{6,7},{7,6},{8,9},{9,8},{10,11... | collective-permute-start | bytes 3072008 | tf_op jit(solution)/shard_map/ppermute | solution.py:306
  1.4 2.9 %collective-permute-start = (bf16[512,250]{1,0:T(8,128)(2,1)}, bf16[512,250]{1,0:T(8,128)(2,1)S(1)}, u32[]{:S(2)}, u32[]{:S(2)}) collective-permute-start(bf16[512,250]{1,0:T(8,128)(2,1)} %rest_1_.1), channel_id=1, source_target_pairs={{0,1},{1,0},{2,3},{3,2},{4,5},{5,4},{6,7},{7,6},{8,9},{9,8},{10,11... | collective-permute-start | bytes 768008 | tf_op jit(solution)/shard_map/ppermute | solution.py:305
  17.0 17.4 %collective-permute-start.2 = (bf16[16,8,1152]{2,1,0:T(8,128)(2,1)S(1)}, bf16[16,8,1152]{2,1,0:T(8,128)(2,1)S(1)}, u32[]{:S(2)}, u32[]{:S(2)}) collective-permute-start(bf16[16,8,1152]{2,1,0:T(8,128)(2,1)S(1)} %get-tuple-element.34), channel_id=1, source_target_pairs={{0,1},{1,0},{2,3},{3,2},{4,5},{5,4},{6,7},{7,6},{8,9},{9,8},{10,11... | collective-permute-start | bytes 884744 | tf_op jit(solution)/shard_map/ppermute | solution.py:349
  17.4 10.4 %collective-permute-start.3 = (bf16[128,1024]{1,0:T(8,128)(2,1)S(1)}, bf16[128,1024]{1,0:T(8,128)(2,1)S(1)}, u32[]{:S(2)}, u32[]{:S(2)}) collective-permute-start(bf16[128,1024]{1,0:T(8,128)(2,1)S(1)} %get-tuple-element.36), channel_id=1, source_target_pairs={{0,32},{32,64},{64,96},{96,0},{1,33},{33,65},{65,97},{97,1},{2,34}... | collective-permute-start | bytes 786440 | tf_op jit(solution)/shard_map/ppermute | solution.py:327
  19.2 15.2 %collective-permute-start.4 = (bf16[128,1024]{1,0:T(8,128)(2,1)S(1)}, bf16[128,1024]{1,0:T(8,128)(2,1)S(1)}, u32[]{:S(2)}, u32[]{:S(2)}) collective-permute-start(bf16[128,1024]{1,0:T(8,128)(2,1)S(1)} %get-tuple-element.37), channel_id=1, source_target_pairs={{0,64},{32,96},{64,0},{96,32},{1,65},{33,97},{65,1},{97,33},{2,66}... | collective-permute-start | bytes 786440 | tf_op jit(solution)/shard_map/ppermute | solution.py:327
  22.5 11.9 %collective-permute-start.5 = (bf16[128,1024]{1,0:T(8,128)(2,1)S(1)}, bf16[128,1024]{1,0:T(8,128)(2,1)S(1)}, u32[]{:S(2)}, u32[]{:S(2)}) collective-permute-start(bf16[128,1024]{1,0:T(8,128)(2,1)S(1)} %get-tuple-element.38), channel_id=1, source_target_pairs={{0,96},{32,0},{64,32},{96,64},{1,97},{33,1},{65,33},{97,65},{2,98}... | collective-permute-start | bytes 786440 | tf_op jit(solution)/shard_map/ppermute | solution.py:327
  34.4 33.3 %copy-start.1 = (s32[128]{0:T(128)S(1)}, s32[128]{0:T(128)}, u32[]{:S(2)}) copy-start(s32[128]{0:T(128)} %param.13) | copy-start | bytes 1540
  62.9 4.8 %collective-permute-start.6 = (bf16[16,8,1152]{2,1,0:T(8,128)(2,1)S(1)}, bf16[16,8,1152]{2,1,0:T(8,128)(2,1)S(1)}, u32[]{:S(2)}, u32[]{:S(2)}) collective-permute-start(bf16[16,8,1152]{2,1,0:T(8,128)(2,1)S(1)} %all_to_all.31.mine_gap_ref), channel_id=1, source_target_pairs={{0,1},{1,0},{2,3},{3,2},{4,5},{5,4},{6,7},{7,6},{8,9},{9,8},{10,11... | collective-permute-start | bytes 884744 | tf_op jit(solution)/shard_map/ppermute | solution.py:379
  72.7 2.3 %collective-permute-start.7 = (bf16[16,8,1152]{2,1,0:T(8,128)(2,1)S(1)}, bf16[16,8,1152]{2,1,0:T(8,128)(2,1)S(1)}, u32[]{:S(2)}, u32[]{:S(2)}) collective-permute-start(bf16[16,8,1152]{2,1,0:T(8,128)(2,1)S(1)} %get-tuple-element.43.other_ref), channel_id=1, source_target_pairs={{0,1},{1,0},{2,3},{3,2},{4,5},{5,4},{6,7},{7,6},{8,9},{9,8},{10,11... | collective-permute-start | bytes 884744 | tf_op jit(solution)/shard_map/ppermute | solution.py:349
  98.0 3.9 %collective-permute-start.8 = (bf16[16,8,1152]{2,1,0:T(8,128)(2,1)S(1)}, bf16[16,8,1152]{2,1,0:T(8,128)(2,1)S(1)}, u32[]{:S(2)}, u32[]{:S(2)}) collective-permute-start(bf16[16,8,1152]{2,1,0:T(8,128)(2,1)S(1)} %all_to_all.33.mine_gap_ref), channel_id=1, source_target_pairs={{0,1},{1,0},{2,3},{3,2},{4,5},{5,4},{6,7},{7,6},{8,9},{9,8},{10,11... | collective-permute-start | bytes 884744 | tf_op jit(solution)/shard_map/ppermute | solution.py:379
  107.1 2.5 %collective-permute-start.9 = (bf16[16,8,1152]{2,1,0:T(8,128)(2,1)S(1)}, bf16[16,8,1152]{2,1,0:T(8,128)(2,1)S(1)}, u32[]{:S(2)}, u32[]{:S(2)}) collective-permute-start(bf16[16,8,1152]{2,1,0:T(8,128)(2,1)S(1)} %get-tuple-element.47.other_ref), channel_id=1, source_target_pairs={{0,1},{1,0},{2,3},{3,2},{4,5},{5,4},{6,7},{7,6},{8,9},{9,8},{10,11... | collective-permute-start | bytes 884744 | tf_op jit(solution)/shard_map/ppermute | solution.py:349
  132.5 3.9 %collective-permute-start.10 = (bf16[16,8,1152]{2,1,0:T(8,128)(2,1)S(1)}, bf16[16,8,1152]{2,1,0:T(8,128)(2,1)S(1)}, u32[]{:S(2)}, u32[]{:S(2)}) collective-permute-start(bf16[16,8,1152]{2,1,0:T(8,128)(2,1)S(1)} %all_to_all.35.mine_gap_ref), channel_id=1, source_target_pairs={{0,1},{1,0},{2,3},{3,2},{4,5},{5,4},{6,7},{7,6},{8,9},{9,8},{10,11... | collective-permute-start | bytes 884744 | tf_op jit(solution)/shard_map/ppermute | solution.py:379

commit v5 on v4

--- a/solution.py
+++ b/solution.py
@@ -197,20 +197,31 @@
     out_ref[:, :, half:] = jnp.broadcast_to(tile[None], (in_ref.shape[0],) + tile.shape)
 
 
-def step_kernel(last, place_ref, mine_gap_ref, other_gap_ref, active_ref, base_ref, update_ref, turned_ref, *rest):
+def near_kernel(place_ref, gap_ref, turned_ref, *rest):
+    part_ref = rest[-1]
+    rows = part_ref.shape[0]
+    half = gap_ref.shape[2] - LANES
+    piece = gap_ref[:, :, :half].astype(jnp.float32).reshape(rows, half).astype(jnp.bfloat16)
+    depth = pl.ds(pl.multiple_of(place_ref[1] * half, half), half)
+    for start in range(0, turned_ref.shape[1], CHUNK):
+        where = pl.ds(start, CHUNK)
+        part_ref[:, where] = jnp.dot(piece, turned_ref[depth, where], preferred_element_type=jnp.float32)
+
+
+def step_kernel(last, place_ref, mine_gap_ref, other_gap_ref, part_ref, active_ref, base_ref, update_ref, turned_ref, *rest):
     if last:
-        out_ref, new_ref, gap_all, sems = rest
+        out_ref, new_ref, sems = rest
     else:
-        held_ref, new_ref, weights_ref, other_ref, gap_all, logits_ref, mass_ref = rest
+        held_ref, new_ref, weights_ref, other_ref, logits_ref, mass_ref = rest
     extent, rows = base_ref.shape
     half = mine_gap_ref.shape[2] - LANES
     core = place_ref[1]
-    stats = []
-    for gap_ref, which in ((mine_gap_ref, core), (other_gap_ref, 1 - core)):
-        columns = pl.ds(pl.multiple_of(which * half, half), half)
-        piece = gap_ref[:, :, :half].astype(jnp.float32).reshape(rows, half)
-        gap_all[:, columns] = piece.astype(jnp.bfloat16)
-        stats.append(gap_ref[:, :, half:].astype(jnp.float32).reshape(rows, LANES).T)
+    stats = [ref[:, :, half:].astype(jnp.float32).reshape(rows, LANES).T for ref in (mine_gap_ref, other_gap_ref)]
+    piece = other_gap_ref[:, :, :half].astype(jnp.float32).reshape(rows, half).astype(jnp.bfloat16)
+    depth = pl.ds(pl.multiple_of((1 - core) * half, half), half)
+    if part_ref is None:
+        own_piece = mine_gap_ref[:, :, :half].astype(jnp.float32).reshape(rows, half).astype(jnp.bfloat16)
+        own_depth = pl.ds(pl.multiple_of(core * half, half), half)
 
     def joined(which, h):
         return jnp.sum(stats[h][3 * which : 3 * which + 3], axis=0, keepdims=True)
@@ -224,8 +235,12 @@
     copies = []
     for start, size in chunks_of(extent):
         where = pl.ds(start, size)
-        turned = jnp.dot(gap_all[...], turned_ref[:, start : start + size], preferred_element_type=jnp.float32)
-        back = turned.T * scale
+        part = jnp.dot(piece, turned_ref[depth, start : start + size], preferred_element_type=jnp.float32)
+        if part_ref is None:
+            near = jnp.dot(own_piece, turned_ref[own_depth, start : start + size], preferred_element_type=jnp.float32)
+        else:
+            near = part_ref[:, start : start + size]
+        back = (near + part).T * scale
         logits = base_ref[where, :]
         if update_ref is not None:
             logits = logits + update_ref[where, :]
@@ -246,7 +261,7 @@
 
 def no_update(kernel):
     def run(place_ref, mine_gap_ref, other_gap_ref, active_ref, base_ref, turned_ref, *rest):
-        kernel(place_ref, mine_gap_ref, other_gap_ref, active_ref, base_ref, None, turned_ref, *rest)
+        kernel(place_ref, mine_gap_ref, other_gap_ref, None, active_ref, base_ref, None, turned_ref, *rest)
 
     return run
 
@@ -330,6 +345,7 @@
     held_shape = pltpu.VMEM((base_width, anchors), bf16)
     turned_shape = pltpu.VMEM((anchors, -(-base_width // LANES) * LANES), bf16)
     weights_shape = jax.ShapeDtypeStruct((rows, -(-base_width // LANES) * LANES), bf16)
+    part_shape = jax.ShapeDtypeStruct((rows, -(-base_width // LANES) * LANES), f32)
     update_shape = jax.ShapeDtypeStruct((base_width, rows), f32)
     held, turned, mine, other = pl.pallas_call(
         first_kernel,
@@ -377,15 +393,27 @@
             copies = result
         gaps = lax.all_to_all(copies, CHIPS[1:], 0, 0, tiled=True)
         other_gaps = lax.ppermute(gaps, "core", swap)
+        if update is None:
+            parts = []
+        else:
+            kept = [base, update] + ([] if last else [held])
+            part = pl.pallas_call(
+                near_kernel,
+                out_shape=part_shape,
+                in_specs=[SMEM, VMEM, VMEM] + [HBM] * len(kept),
+                out_specs=VMEM,
+                compiler_params=grant(3),
+                name="near_half",
+            )(base_place, gaps, turned, *kept)
+            parts = [part]
         kernel = functools.partial(step_kernel, last)
-        operands = [base_place, gaps, other_gaps, active, base] + ([] if update is None else [update]) + [turned] + ([] if last else [held])
+        operands = [base_place, gaps, other_gaps, *parts, active, base] + ([] if update is None else [update]) + [turned] + ([] if last else [held])
         result = pl.pallas_call(
             no_update(kernel) if update is None else kernel,
             out_shape=update_shape if last else (update_shape, weights_shape, sent_shape),
             in_specs=[SMEM] + [VMEM] * (len(operands) - 1),
             out_specs=HBM if last else (VMEM, VMEM, VMEM),
             scratch_shapes=([pltpu.VMEM((base_width, rows), f32)] if last else [])
-            + [pltpu.VMEM((rows, anchors), bf16)]
             + (
                 [pltpu.SemaphoreType.DMA((pieces,))]
                 if last

time: 141 us -> 140 us (level)
  waiting for transfers between devices: 17.5 us -> 15.1 us
  Pallas kernels: 32.6 us -> 34.3 us
    pallas_call x0 -> x2, Pallas kernels: none -> 3.67 us  [shards(): pl.pallas_call(near_kernel, out_shape=part_shape, in_specs=[SMEM, VMEM, V...]
    ppermute x3, waiting for transfers between devices: 3.63 us -> 1.21 us  [shards(): other_gaps = lax.ppermute(gaps, 'core', swap)]
    pallas_call x3, Pallas kernels: 14.6 us -> 12.6 us  [shards(): pl.pallas_call(no_update(kernel) if update is None else kernel, out_shape...]
  transfers between devices with their start and end apart: 11 -> 11, of which waited for: 6 -> 4; matrix products, arithmetic and copies ran while one was open for 0% -> 0% of each run, Pallas kernels for 3% -> 5%
where the time goes in v5:
time: 140 us
  blocking collectives  72.1 us (51%)
  Pallas kernels  34.3 us (24%)
  starting transfers between devices  17.7 us (13%)
  waiting for transfers between devices  15.1 us (11%)
    all_to_all x3, blocking collectives, shards(): got = lax.all_to_all(sent, CHIPS[1:], 0, 0, tiled=True)  38.9 us
    all_to_all x3, blocking collectives, shards(): gaps = lax.all_to_all(copies, CHIPS[1:], 0, 0, tiled=True)  33.2 us
    pallas_call x3, Pallas kernels, shards(): pl.pallas_call(no_update(kernel) if update is None else kernel, out_shape...  12.6 us
    ppermute x3, waiting for transfers between devices, shards(): targets[far] = lax.ppermute(targets[far], 'rows', ring)  11.1 us
    pallas_call x1, Pallas kernels, shards(): pl.pallas_call(first_kernel, out_shape=(held_shape, turned_shape, sent_sh...  9.51 us
    ppermute x3, starting transfers between devices, shards(): other_gaps = lax.ppermute(gaps, 'core', swap)  9.32 us
    ppermute x3, starting transfers between devices, shards(): targets[far] = lax.ppermute(targets[far], 'rows', ring)  5.79 us
    pallas_call x2, Pallas kernels, shards(): pl.pallas_call(near_kernel, out_shape=part_shape, in_specs=[SMEM, VMEM, V...  3.67 us
  transfers between devices with their start and end apart: 11, of which 4 were waited for; matrix products, arithmetic and copies ran while one was open for 0% of the time, Pallas kernels for 5%

profile of v5, /device:TPU:1, one launch (start us, length us, event | category | flops | bytes accessed | tf_op | source)
XLA Modules:
  0.0 139.7 jit_solution(11990930157546171003)
XLA Ops:
  0.0 0.0 copy-start.3
  0.0 1.4 collective-permute-start.1
  1.4 0.0 collective-permute-start
  1.4 0.0 copy-start
  1.4 0.1 pad_add_fusion.place_ref
  1.5 0.1 pad_add_fusion.1.place_ref
  1.5 2.7 %collective-permute-done.rest_3_ = bf16[512,250]{1,0:T(8,128)(2,1)S(1)} collective-permute-done((bf16[512,250]{1,0:T(8,128)(2,1)}, bf16[512,250]{1,0:T(8,128)(2,1)S(1)}, u32[]{:S(2)}, u32[]{:S(2)}) %collective-permute-start) | collective-permute-done | bytes 256032 | tf_op jit(solution)/shard_map/ppermute | solution.py:320
  4.3 0.0 collective-permute-done.1.rest_4_
  4.3 3.2 %target_parts.1 = (bf16[128,1024]{1,0:T(8,128)(2,1)S(1)}, bf16[128,1024]{1,0:T(8,128)(2,1)S(1)}, bf16[128,1024]{1,0:T(8,128)(2,1)S(1)}, bf16[128,1024]{1,0:T(8,128)(2,1)S(1)}) custom-call(s32[4]{0:T(128)S(1)} %pad_add_fusion.1.place_ref, s32[1,2048]{1,0:T(1,128)} %bitcast.20, bf16[512,250]{1,0:T(8,128)(2,1)} %rest_1_.1, bf16[250,2048]{1,0:T(8,128)(2,1)} %rest_2_.1, ...), custom_call_target="tpu_custom_call" | custom-call | tf_op jit(solution)/shard_map/target_parts/pallas_call | solution.py:323
  7.4 0.0 copy-done.3
  7.4 0.0 copy-done
  7.5 9.5 %first_masses.1 = (bf16[4008,2048]{1,0:T(8,128)(2,1)S(1)}, bf16[2048,4096]{1,0:T(8,128)(2,1)S(1)}, bf16[16,8,1152]{2,1,0:T(8,128)(2,1)S(1)}, bf16[16,8,1152]{2,1,0:T(8,128)(2,1)S(1)}) custom-call(s32[2]{0:T(128)S(1)} %pad_add_fusion.place_ref, s32[1,2048]{1,0:T(1,128)S(1)} %bitcast.19, bf16[4008,2048]{1,0:T(8,128)(2,1)} %anchors_ref.1, f32[4008,128]{1,0:T(8,128)S(1)} %bitcast.10), custom_call_target="tpu_custom_call" | custom-call | flops 8000000000 | bytes 40000000 | tf_op jit(solution)/shard_map/first_masses/pallas_call | solution.py:350
  17.0 0.5 collective-permute-start.2
  17.4 1.8 %collective-permute-start.3 = (bf16[128,1024]{1,0:T(8,128)(2,1)S(1)}, bf16[128,1024]{1,0:T(8,128)(2,1)S(1)}, u32[]{:S(2)}, u32[]{:S(2)}) collective-permute-start(bf16[128,1024]{1,0:T(8,128)(2,1)S(1)} %get-tuple-element.36), channel_id=1, source_target_pairs={{0,32},{32,64},{64,96},{96,0},{1,33},{33,65},{65,97},{97,1},{2,34}... | collective-permute-start | bytes 786440 | tf_op jit(solution)/shard_map/ppermute | solution.py:342
  19.2 3.3 %collective-permute-start.4 = (bf16[128,1024]{1,0:T(8,128)(2,1)S(1)}, bf16[128,1024]{1,0:T(8,128)(2,1)S(1)}, u32[]{:S(2)}, u32[]{:S(2)}) collective-permute-start(bf16[128,1024]{1,0:T(8,128)(2,1)S(1)} %get-tuple-element.37), channel_id=1, source_target_pairs={{0,64},{32,96},{64,0},{96,32},{1,65},{33,97},{65,1},{97,33},{2,66}... | collective-permute-start | bytes 786440 | tf_op jit(solution)/shard_map/ppermute | solution.py:342
  22.5 0.7 collective-permute-start.5
  23.2 4.6 %collective-permute-done.3.rest_1_ = bf16[128,1024]{1,0:T(8,128)(2,1)S(1)} collective-permute-done((bf16[128,1024]{1,0:T(8,128)(2,1)S(1)}, bf16[128,1024]{1,0:T(8,128)(2,1)S(1)}, u32[]{:S(2)}, u32[]{:S(2)}) %collective-permute-start.3) | collective-permute-done | bytes 262176 | tf_op jit(solution)/shard_map/ppermute | solution.py:342
  27.8 6.5 %collective-permute-done.4.rest_2_ = bf16[128,1024]{1,0:T(8,128)(2,1)S(1)} collective-permute-done((bf16[128,1024]{1,0:T(8,128)(2,1)S(1)}, bf16[128,1024]{1,0:T(8,128)(2,1)S(1)}, u32[]{:S(2)}, u32[]{:S(2)}) %collective-permute-start.4) | collective-permute-done | bytes 262176 | tf_op jit(solution)/shard_map/ppermute | solution.py:342
  34.4 0.0 collective-permute-done.5.rest_3_
  34.4 0.0 collective-permute-done.2.other_ref
  34.4 0.0 copy-start.2
  34.4 0.5 pair.3
  34.8 17.0 %all_to_all.30.in_ref = bf16[16,8,2176]{2,1,0:T(8,128)(2,1)S(1)} all-to-all(bf16[16,8,2176]{2,1,0:T(8,128)(2,1)S(1)} %pair.3), channel_id=1, replica_groups=mesh['rows'=4,'x'=4,'y'=4,'core'=2] {'x','y'}, dimensions={0} | all-to-all | bytes 1114112 | tf_op jit(solution)/shard_map/all_to_all | solution.py:379
  51.8 0.3 owner.3
  52.1 10.8 %all_to_all.31.mine_gap_ref = bf16[16,8,1152]{2,1,0:T(8,128)(2,1)S(1)} all-to-all(bf16[16,8,1152]{2,1,0:T(8,128)(2,1)S(1)} %get-tuple-element.39), channel_id=1, replica_groups=mesh['rows'=4,'x'=4,'y'=4,'core'=2] {'x','y'}, dimensions={0} | all-to-all | bytes 589824 | tf_op jit(solution)/shard_map/all_to_all | solution.py:394
  62.9 3.6 %collective-permute-start.6 = (bf16[16,8,1152]{2,1,0:T(8,128)(2,1)S(1)}, bf16[16,8,1152]{2,1,0:T(8,128)(2,1)S(1)}, u32[]{:S(2)}, u32[]{:S(2)}) collective-permute-start(bf16[16,8,1152]{2,1,0:T(8,128)(2,1)S(1)} %all_to_all.31.mine_gap_ref), channel_id=1, source_target_pairs={{0,1},{1,0},{2,3},{3,2},{4,5},{5,4},{6,7},{7,6},{8,9},{9,8},{10,11... | collective-permute-start | bytes 884744 | tf_op jit(solution)/shard_map/ppermute | solution.py:395
  66.4 1.2 collective-permute-done.6.other_gap_ref
  67.6 0.0 copy-done.2
  67.6 5.0 %step.3 = (f32[4008,128]{1,0:T(8,128)S(1)}, bf16[128,4096]{1,0:T(8,128)(2,1)S(1)}, bf16[16,8,1152]{2,1,0:T(8,128)(2,1)S(1)}) custom-call(s32[2]{0:T(128)S(1)} %pad_add_fusion.place_ref, bf16[16,8,1152]{2,1,0:T(8,128)(2,1)S(1)} %all_to_all.31.mine_gap_ref, bf16[16,8,1152]{2,1,0:T(8,128)(2,1)S(1)} %collective-permute-done.6.other_gap_ref, ...), custom_call_target="tpu_custom_call" | custom-call | tf_op jit(solution)/shard_map/step/pallas_call | solution.py:411
  72.6 0.5 collective-permute-start.7
  73.1 1.8 %own_half.2.mine_ref = bf16[16,8,1152]{2,1,0:T(8,128)(2,1)S(1)} custom-call(s32[2]{0:T(128)S(1)} %pad_add_fusion.place_ref, bf16[128,4096]{1,0:T(8,128)(2,1)S(1)} %get-tuple-element.42.weights_ref, bf16[4008,2048]{1,0:T(8,128)(2,1)S(1)} %get-tuple-element.41.rest_0_.held_ref.rest_2_, bf16[16,8,1152]{2,1,0:T(8,128)(2,1)S(1)} %get-tuple-element.43.other_ref, ...), custom_call_target="tpu_custom_call" | custom-call | tf_op jit(solution)/shard_map/own_half/pallas_call | solution.py:429
  74.9 0.0 collective-permute-done.7.other_ref
  74.9 0.3 pair.4
  75.2 11.1 %all_to_all.32.in_ref = bf16[16,8,1152]{2,1,0:T(8,128)(2,1)S(1)} all-to-all(bf16[16,8,1152]{2,1,0:T(8,128)(2,1)S(1)} %pair.4), channel_id=1, replica_groups=mesh['rows'=4,'x'=4,'y'=4,'core'=2] {'x','y'}, dimensions={0} | all-to-all | bytes 589824 | tf_op jit(solution)/shard_map/all_to_all | solution.py:379
  86.3 0.3 owner.4
  86.5 11.3 %all_to_all.33.gap_ref.mine_gap_ref = bf16[16,8,1152]{2,1,0:T(8,128)(2,1)S(1)} all-to-all(bf16[16,8,1152]{2,1,0:T(8,128)(2,1)S(1)} %owner.4), channel_id=1, replica_groups=mesh['rows'=4,'x'=4,'y'=4,'core'=2] {'x','y'}, dimensions={0} | all-to-all | bytes 589824 | tf_op jit(solution)/shard_map/all_to_all | solution.py:394
  97.8 2.7 %collective-permute-start.8 = (bf16[16,8,1152]{2,1,0:T(8,128)(2,1)S(1)}, bf16[16,8,1152]{2,1,0:T(8,128)(2,1)S(1)}, u32[]{:S(2)}, u32[]{:S(2)}) collective-permute-start(bf16[16,8,1152]{2,1,0:T(8,128)(2,1)S(1)} %all_to_all.33.gap_ref.mine_gap_ref), channel_id=1, source_target_pairs={{0,1},{1,0},{2,3},{3,2},{4,5},{5,4},{6,7},{7,6},{8,9},{9,8},{10,11... | collective-permute-start | bytes 884744 | tf_op jit(solution)/shard_map/ppermute | solution.py:395
  100.5 0.0 copy-start.1
  100.5 1.8 %near_half.2.part_ref = f32[128,4096]{1,0:T(8,128)S(1)} custom-call(s32[2]{0:T(128)S(1)} %pad_add_fusion.place_ref, bf16[16,8,1152]{2,1,0:T(8,128)(2,1)S(1)} %all_to_all.33.gap_ref.mine_gap_ref, bf16[2048,4096]{1,0:T(8,128)(2,1)S(1)} %get-tuple-element.40.turned_ref, f32[4008,128]{1,0:T(8,128)S(1)} %bitcast.12, ...), custom_call_target="tpu_custom_call" | custom-call | tf_op jit(solution)/shard_map/near_half/pallas_call | solution.py:400
  102.3 0.0 collective-permute-done.8.other_gap_ref
  102.4 0.0 copy-done.1
  102.4 4.3 %step.4 = (f32[4008,128]{1,0:T(8,128)S(1)}, bf16[128,4096]{1,0:T(8,128)(2,1)S(1)}, bf16[16,8,1152]{2,1,0:T(8,128)(2,1)S(1)}) custom-call(s32[2]{0:T(128)S(1)} %pad_add_fusion.place_ref, bf16[16,8,1152]{2,1,0:T(8,128)(2,1)S(1)} %all_to_all.33.gap_ref.mine_gap_ref, bf16[16,8,1152]{2,1,0:T(8,128)(2,1)S(1)} %collective-permute-done.8.other_gap_ref, ...), custom_call_target="tpu_custom_call" | custom-call | tf_op jit(solution)/shard_map/step/pallas_call | solution.py:411
  106.7 0.3 collective-permute-start.9
  107.0 1.8 %own_half.3.mine_ref = bf16[16,8,1152]{2,1,0:T(8,128)(2,1)S(1)} custom-call(s32[2]{0:T(128)S(1)} %pad_add_fusion.place_ref, bf16[128,4096]{1,0:T(8,128)(2,1)S(1)} %get-tuple-element.46.weights_ref, bf16[4008,2048]{1,0:T(8,128)(2,1)S(1)} %get-tuple-element.41.rest_0_.held_ref.rest_2_, bf16[16,8,1152]{2,1,0:T(8,128)(2,1)S(1)} %get-tuple-element.47.other_ref, ...), custom_call_target="tpu_custom_call" | custom-call | tf_op jit(solution)/shard_map/own_half/pallas_call | solution.py:429
  108.8 0.0 collective-permute-done.9.other_ref
  108.8 0.3 pair.5
  109.1 10.8 %all_to_all.34.in_ref = bf16[16,8,1152]{2,1,0:T(8,128)(2,1)S(1)} all-to-all(bf16[16,8,1152]{2,1,0:T(8,128)(2,1)S(1)} %pair.5), channel_id=1, replica_groups=mesh['rows'=4,'x'=4,'y'=4,'core'=2] {'x','y'}, dimensions={0} | all-to-all | bytes 589824 | tf_op jit(solution)/shard_map/all_to_all | solution.py:379
  119.9 0.3 owner.5
  120.2 11.2 %all_to_all.35.gap_ref.mine_gap_ref = bf16[16,8,1152]{2,1,0:T(8,128)(2,1)S(1)} all-to-all(bf16[16,8,1152]{2,1,0:T(8,128)(2,1)S(1)} %owner.5), channel_id=1, replica_groups=mesh['rows'=4,'x'=4,'y'=4,'core'=2] {'x','y'}, dimensions={0} | all-to-all | bytes 589824 | tf_op jit(solution)/shard_map/all_to_all | solution.py:394
  131.4 3.1 %collective-permute-start.10 = (bf16[16,8,1152]{2,1,0:T(8,128)(2,1)S(1)}, bf16[16,8,1152]{2,1,0:T(8,128)(2,1)S(1)}, u32[]{:S(2)}, u32[]{:S(2)}) collective-permute-start(bf16[16,8,1152]{2,1,0:T(8,128)(2,1)S(1)} %all_to_all.35.gap_ref.mine_gap_ref), channel_id=1, source_target_pairs={{0,1},{1,0},{2,3},{3,2},{4,5},{5,4},{6,7},{7,6},{8,9},{9,8},{10,11... | collective-permute-start | bytes 884744 | tf_op jit(solution)/shard_map/ppermute | solution.py:395
  134.4 1.9 %near_half.3.part_ref = f32[128,4096]{1,0:T(8,128)S(1)} custom-call(s32[2]{0:T(128)S(1)} %pad_add_fusion.place_ref, bf16[16,8,1152]{2,1,0:T(8,128)(2,1)S(1)} %all_to_all.35.gap_ref.mine_gap_ref, bf16[2048,4096]{1,0:T(8,128)(2,1)S(1)} %get-tuple-element.40.turned_ref, f32[4008,128]{1,0:T(8,128)S(1)} %bitcast.14, ...), custom_call_target="tpu_custom_call" | custom-call | tf_op jit(solution)/shard_map/near_half/pallas_call | solution.py:400
  136.3 0.0 collective-permute-done.10.other_gap_ref
  136.3 3.3 %step.5 = f32[4008,128]{1,0:T(8,128)} custom-call(s32[2]{0:T(128)S(1)} %pad_add_fusion.place_ref, bf16[16,8,1152]{2,1,0:T(8,128)(2,1)S(1)} %all_to_all.35.gap_ref.mine_gap_ref, bf16[16,8,1152]{2,1,0:T(8,128)(2,1)S(1)} %collective-permute-done.10.other_gap_ref, f32[128,4096]{1,0:T(8,128)S(1)} %near_half.3.part_ref, s32[1,128]{1,0:T(1,128)S(1)} %bitcast.18, ...), custom_call_target="tpu_custom_call" | custom-call | tf_op jit(solution)/shard_map/step/pallas_call | solution.py:411
Async XLA Ops:
  0.0 7.4 %copy-start.3 = (s32[2048]{0:T(1024)S(1)}, s32[2048]{0:T(1024)}, u32[]{:S(2)}) copy-start(s32[2048]{0:T(1024)} %param.12) | copy-start | bytes 24580
  0.0 4.3 %collective-permute-start.1 = (bf16[250,2048]{1,0:T(8,128)(2,1)}, bf16[250,2048]{1,0:T(8,128)(2,1)S(1)}, u32[]{:S(2)}, u32[]{:S(2)}) collective-permute-start(bf16[250,2048]{1,0:T(8,128)(2,1)} %rest_2_.1), channel_id=1, source_target_pairs={{0,1},{1,0},{2,3},{3,2},{4,5},{5,4},{6,7},{7,6},{8,9},{9,8},{10,11... | collective-permute-start | bytes 3072008 | tf_op jit(solution)/shard_map/ppermute | solution.py:321
  1.4 2.9 %collective-permute-start = (bf16[512,250]{1,0:T(8,128)(2,1)}, bf16[512,250]{1,0:T(8,128)(2,1)S(1)}, u32[]{:S(2)}, u32[]{:S(2)}) collective-permute-start(bf16[512,250]{1,0:T(8,128)(2,1)} %rest_1_.1), channel_id=1, source_target_pairs={{0,1},{1,0},{2,3},{3,2},{4,5},{5,4},{6,7},{7,6},{8,9},{9,8},{10,11... | collective-permute-start | bytes 768008 | tf_op jit(solution)/shard_map/ppermute | solution.py:320
  1.4 6.1 %copy-start = (f32[128,4008]{0,1:T(8,128)S(1)}, f32[128,4008]{0,1:T(8,128)}, u32[]{:S(2)}) copy-start(f32[128,4008]{0,1:T(8,128)} %param.10) | copy-start | bytes 6156292
  17.0 17.4 %collective-permute-start.2 = (bf16[16,8,1152]{2,1,0:T(8,128)(2,1)S(1)}, bf16[16,8,1152]{2,1,0:T(8,128)(2,1)S(1)}, u32[]{:S(2)}, u32[]{:S(2)}) collective-permute-start(bf16[16,8,1152]{2,1,0:T(8,128)(2,1)S(1)} %get-tuple-element.34), channel_id=1, source_target_pairs={{0,1},{1,0},{2,3},{3,2},{4,5},{5,4},{6,7},{7,6},{8,9},{9,8},{10,11... | collective-permute-start | bytes 884744 | tf_op jit(solution)/shard_map/ppermute | solution.py:365
  17.4 10.4 %collective-permute-start.3 = (bf16[128,1024]{1,0:T(8,128)(2,1)S(1)}, bf16[128,1024]{1,0:T(8,128)(2,1)S(1)}, u32[]{:S(2)}, u32[]{:S(2)}) collective-permute-start(bf16[128,1024]{1,0:T(8,128)(2,1)S(1)} %get-tuple-element.36), channel_id=1, source_target_pairs={{0,32},{32,64},{64,96},{96,0},{1,33},{33,65},{65,97},{97,1},{2,34}... | collective-permute-start | bytes 786440 | tf_op jit(solution)/shard_map/ppermute | solution.py:342
  19.2 15.2 %collective-permute-start.4 = (bf16[128,1024]{1,0:T(8,128)(2,1)S(1)}, bf16[128,1024]{1,0:T(8,128)(2,1)S(1)}, u32[]{:S(2)}, u32[]{:S(2)}) collective-permute-start(bf16[128,1024]{1,0:T(8,128)(2,1)S(1)} %get-tuple-element.37), channel_id=1, source_target_pairs={{0,64},{32,96},{64,0},{96,32},{1,65},{33,97},{65,1},{97,33},{2,66}... | collective-permute-start | bytes 786440 | tf_op jit(solution)/shard_map/ppermute | solution.py:342
  22.5 11.9 %collective-permute-start.5 = (bf16[128,1024]{1,0:T(8,128)(2,1)S(1)}, bf16[128,1024]{1,0:T(8,128)(2,1)S(1)}, u32[]{:S(2)}, u32[]{:S(2)}) collective-permute-start(bf16[128,1024]{1,0:T(8,128)(2,1)S(1)} %get-tuple-element.38), channel_id=1, source_target_pairs={{0,96},{32,0},{64,32},{96,64},{1,97},{33,1},{65,33},{97,65},{2,98}... | collective-permute-start | bytes 786440 | tf_op jit(solution)/shard_map/ppermute | solution.py:342
  34.4 33.3 %copy-start.2 = (s32[128]{0:T(128)S(1)}, s32[128]{0:T(128)}, u32[]{:S(2)}) copy-start(s32[128]{0:T(128)} %param.13) | copy-start | bytes 1540
  62.9 4.8 %collective-permute-start.6 = (bf16[16,8,1152]{2,1,0:T(8,128)(2,1)S(1)}, bf16[16,8,1152]{2,1,0:T(8,128)(2,1)S(1)}, u32[]{:S(2)}, u32[]{:S(2)}) collective-permute-start(bf16[16,8,1152]{2,1,0:T(8,128)(2,1)S(1)} %all_to_all.31.mine_gap_ref), channel_id=1, source_target_pairs={{0,1},{1,0},{2,3},{3,2},{4,5},{5,4},{6,7},{7,6},{8,9},{9,8},{10,11... | collective-permute-start | bytes 884744 | tf_op jit(solution)/shard_map/ppermute | solution.py:395
  72.6 2.3 %collective-permute-start.7 = (bf16[16,8,1152]{2,1,0:T(8,128)(2,1)S(1)}, bf16[16,8,1152]{2,1,0:T(8,128)(2,1)S(1)}, u32[]{:S(2)}, u32[]{:S(2)}) collective-permute-start(bf16[16,8,1152]{2,1,0:T(8,128)(2,1)S(1)} %get-tuple-element.43.other_ref), channel_id=1, source_target_pairs={{0,1},{1,0},{2,3},{3,2},{4,5},{5,4},{6,7},{7,6},{8,9},{9,8},{10,11... | collective-permute-start | bytes 884744 | tf_op jit(solution)/shard_map/ppermute | solution.py:365
  97.8 4.5 %collective-permute-start.8 = (bf16[16,8,1152]{2,1,0:T(8,128)(2,1)S(1)}, bf16[16,8,1152]{2,1,0:T(8,128)(2,1)S(1)}, u32[]{:S(2)}, u32[]{:S(2)}) collective-permute-start(bf16[16,8,1152]{2,1,0:T(8,128)(2,1)S(1)} %all_to_all.33.gap_ref.mine_gap_ref), channel_id=1, source_target_pairs={{0,1},{1,0},{2,3},{3,2},{4,5},{5,4},{6,7},{7,6},{8,9},{9,8},{10,11... | collective-permute-start | bytes 884744 | tf_op jit(solution)/shard_map/ppermute | solution.py:395
  100.5 1.8 %copy-start.1 = (f32[128,4008]{0,1:T(8,128)S(1)}, f32[128,4008]{0,1:T(8,128)}, u32[]{:S(2)}) copy-start(f32[128,4008]{0,1:T(8,128)} %param.10) | copy-start | bytes 6156292
  106.7 2.1 %collective-permute-start.9 = (bf16[16,8,1152]{2,1,0:T(8,128)(2,1)S(1)}, bf16[16,8,1152]{2,1,0:T(8,128)(2,1)S(1)}, u32[]{:S(2)}, u32[]{:S(2)}) collective-permute-start(bf16[16,8,1152]{2,1,0:T(8,128)(2,1)S(1)} %get-tuple-element.47.other_ref), channel_id=1, source_target_pairs={{0,1},{1,0},{2,3},{3,2},{4,5},{5,4},{6,7},{7,6},{8,9},{9,8},{10,11... | collective-permute-start | bytes 884744 | tf_op jit(solution)/shard_map/ppermute | solution.py:365
  131.4 4.9 %collective-permute-start.10 = (bf16[16,8,1152]{2,1,0:T(8,128)(2,1)S(1)}, bf16[16,8,1152]{2,1,0:T(8,128)(2,1)S(1)}, u32[]{:S(2)}, u32[]{:S(2)}) collective-permute-start(bf16[16,8,1152]{2,1,0:T(8,128)(2,1)S(1)} %all_to_all.35.gap_ref.mine_gap_ref), channel_id=1, source_target_pairs={{0,1},{1,0},{2,3},{3,2},{4,5},{5,4},{6,7},{7,6},{8,9},{9,8},{10,11... | collective-permute-start | bytes 884744 | tf_op jit(solution)/shard_map/ppermute | solution.py:395
